TPU v7x, 512 devices: a whole 4x8x8 slice. The times are simulated.
512 devices in a mesh: ctx: 64 (over z, y), head: 8 (over x, core).
Axes of the slice: x: 4, y: 8, z: 8, core: 2. Of those that a mesh axis runs over, the one named last changes fastest.
Arguments:
- token_inputs: bfloat16 [32768, 8192], P(('ctx', 'head')), may hold values from -6 to 6
- state_in: bfloat16 [32768, 128], P(('ctx', 'head')), may hold values from -0.059814453 to 0.059814453
- state_out: bfloat16 [32768, 128], P(('ctx', 'head')), may hold values from -0.5 to 0.5
- log_decay: bfloat16 [32768, 128], P(('ctx', 'head')), may hold values from -1 to 0
- token_codes: int32 [32768], P(('ctx', 'head')), may hold values from 0 to 63
- level_table: bfloat16 [64, 1408], replicated, may hold values from 0.099609375 to 1
- skip_gain: float32 [128], replicated, may hold values from 0.2 to 1
Outputs:
- mixed_output: bfloat16 [32768, 8192], P(('ctx', 'head'))
All inputs are finite; a program needn't handle non-finite values.
Results may differ from a plain program's by a relative error of at most 0.009.
Values may be sent and summed in bfloat16 or wider, within the bound.
A program may use at most 64 MiB of HBM per device.

v0:
```python
import jax
import jax.numpy as jnp
from jax import lax
from jax.sharding import PartitionSpec as P

COUNT_OF_HEADS = 128
HEAD_DIM = 64
SPAN = 64
LEVELS = 11


def swapped(x, axis, apart):
    return lax.ppermute(x, axis, [(i, i ^ 1 << apart) for i in range(lax.axis_size(axis))])


def look_up(token_codes, weight_table):
    one_hot = (
        token_codes[:, None] == jnp.arange(weight_table.shape[0], dtype=jnp.int32)[None, :]
    ).astype(jnp.bfloat16)
    return jnp.dot(one_hot, weight_table, preferred_element_type=jnp.float32).astype(jnp.bfloat16)


def level_onehot(spans, levels):
    span_ids = jnp.arange(spans, dtype=jnp.int32)
    xored = jnp.bitwise_xor(span_ids[:, None], span_ids[None, :])
    level_ids = jnp.zeros((spans, spans), jnp.int32)
    for level_bit in range(max(spans.bit_length() - 1, 0)):
        level_ids = level_ids + (xored >= 1 << level_bit).astype(jnp.int32)
    return (level_ids[:, :, None] == jnp.arange(levels, dtype=jnp.int32)[None, None, :]).astype(
        jnp.float32
    )


def head_local(scores, head_input, head_weights, head_running, onehot, span):
    block_rows = head_input.shape[0]
    spans = block_rows // span
    weight_blocks = head_weights.astype(jnp.float32).reshape(spans, span, -1)
    pair_weights = jnp.einsum(
        "iql,ijl->iqj", weight_blocks, onehot, precision=lax.Precision.HIGHEST
    )
    row_weights = jnp.broadcast_to(
        pair_weights.reshape(block_rows, spans, 1), (block_rows, spans, span)
    ).reshape(block_rows, block_rows)
    position = jnp.arange(block_rows)
    causal = position[:, None] >= position[None, :]
    log_gap = jnp.where(causal, head_running[:, None] - head_running[None, :], 0.0)
    decay_factor = jnp.where(causal, jnp.exp(log_gap), 0.0)
    weight = (row_weights * decay_factor * scores).astype(jnp.bfloat16)
    return jnp.dot(weight, head_input, preferred_element_type=jnp.float32)


def head_state(head_input, head_running, state_in):
    carried = jnp.exp(head_running[-1] - head_running)[:, None] * head_input.astype(jnp.float32)
    return jnp.einsum(
        "tn,tp->np", state_in, carried.astype(jnp.bfloat16), preferred_element_type=jnp.float32
    )


def finish(
    local_part,
    head_input,
    head_weights,
    head_running,
    state_out,
    bucket_states,
    skip_value,
    span_bits,
    ctx_bits,
):
    reached = jnp.einsum(
        "tn,mnp->tmp", state_out, bucket_states, preferred_element_type=jnp.float32
    )
    factors = (
        head_weights[:, span_bits + 1 : span_bits + 1 + ctx_bits].astype(jnp.float32)
        * jnp.exp(head_running)[:, None]
    )
    cross_part = jnp.sum(factors[:, :, None] * reached, axis=1)
    return (local_part + cross_part + skip_value * head_input.astype(jnp.float32)).astype(
        jnp.bfloat16
    )


def on_device(token_inputs, state_in, state_out, log_decay, token_codes, level_table, skip_gain):
    head_ways = lax.axis_size("head")
    local_heads = COUNT_OF_HEADS // head_ways
    offset = lax.axis_index("head")
    weights_seq = look_up(token_codes, level_table)
    moved_rows, moved_weights, moved_decay = (
        lax.all_to_all(token_inputs, "head", split_axis=1, concat_axis=0, tiled=True),
        lax.all_to_all(weights_seq, "head", split_axis=1, concat_axis=0, tiled=True),
        lax.all_to_all(log_decay, "head", split_axis=1, concat_axis=0, tiled=True),
    )
    in_all, out_all = (
        lax.all_gather(state_in, "head", axis=0, tiled=True),
        lax.all_gather(state_out, "head", axis=0, tiled=True),
    )
    block_rows = moved_rows.shape[0]
    spans = block_rows // SPAN
    span_bits = spans.bit_length() - 1
    input_all = moved_rows.reshape(block_rows, local_heads, HEAD_DIM)
    weights_all = moved_weights.reshape(block_rows, local_heads, LEVELS)
    running = jnp.cumsum(moved_decay.astype(jnp.float32), axis=0)
    onehot = level_onehot(spans, LEVELS)
    scores = jnp.einsum("tn,sn->ts", out_all, in_all, preferred_element_type=jnp.float32)

    def first_pass(head_index):
        head_input = input_all[:, head_index]
        head_running = running[:, head_index]
        local_part = head_local(
            scores, head_input, weights_all[:, head_index], head_running, onehot, SPAN
        )
        return (local_part, head_state(head_input, head_running, in_all))

    local_all, states = lax.map(first_pass, jnp.arange(local_heads))
    summary = states
    summary_decay = running[-1]
    inside = jnp.zeros_like(summary_decay)
    device = lax.axis_index("ctx")
    ctx_bits = lax.axis_size("ctx").bit_length() - 1
    buckets = []
    for level_bit in range(ctx_bits):
        partner, partner_decay = (
            swapped(summary.astype(jnp.bfloat16), "ctx", level_bit).astype(summary.dtype),
            swapped(summary_decay.astype(jnp.bfloat16), "ctx", level_bit).astype(
                summary_decay.dtype
            ),
        )
        is_upper = device >> level_bit & 1 == 1
        buckets.append(
            jnp.where(is_upper, partner * jnp.exp(inside)[:, None, None], 0.0).astype(jnp.bfloat16)
        )
        summary = jnp.where(
            is_upper,
            partner * jnp.exp(summary_decay)[:, None, None] + summary,
            summary * jnp.exp(partner_decay)[:, None, None] + partner,
        )
        inside = jnp.where(is_upper, inside + partner_decay, inside)
        summary_decay = summary_decay + partner_decay
    bucket_stack = jnp.stack(buckets, axis=0)
    gains = lax.dynamic_slice_in_dim(skip_gain, offset * local_heads, local_heads, 0)

    def second_pass(head_index):
        return finish(
            local_all[head_index],
            input_all[:, head_index],
            weights_all[:, head_index],
            running[:, head_index],
            out_all,
            bucket_stack[:, head_index],
            gains[head_index],
            span_bits,
            ctx_bits,
        )

    mixed_rows = lax.map(second_pass, jnp.arange(local_heads))
    merged = jnp.moveaxis(mixed_rows, 0, 1).reshape(block_rows, local_heads * HEAD_DIM)
    return lax.all_to_all(merged, "head", split_axis=0, concat_axis=1, tiled=True)


def solution(mesh):
    return jax.shard_map(
        on_device,
        mesh=mesh,
        in_specs=(
            P(("ctx", "head"), None),
            P(("ctx", "head"), None),
            P(("ctx", "head"), None),
            P(("ctx", "head"), None),
            P(("ctx", "head")),
            P(),
            P(),
        ),
        out_specs=P(("ctx", "head"), None),
        check_vma=False,
    )
```

profile of v0, /device:TPU:1, one launch (start us, length us, event | category | flops | bytes accessed | tf_op | source)
XLA Modules:
  0.0 465.8 jit_solution(6821224827247671395)
XLA Ops:
  1.6 10.1 %all-to-all-start.1 = ((bf16[8,2,512]{2,1,0:T(2,128)(2,1)}), bf16[8,2,512]{2,1,0:T(2,128)(2,1)S(1)}, u32[]{:S(2)}, u32[]{:S(2)}) async-start(bf16[8,2,512]{2,1,0:T(2,128)(2,1)} %reshape.216), calls=%async_computation.1 | async-start | bytes 32768 | tf_op jit(solution)/shard_map/all_to_all | solution.py:91
  11.7 13.7 %all_gather.6 = bf16[512,128]{1,0:T(8,128)(2,1)S(1)} all-gather(bf16[64,128]{1,0:T(8,128)(2,1)} %param.13), channel_id=1, replica_groups=mesh['ctx'=64,'head'=8] {'head'}, dimensions={0}, use_global_device_ids=true | all-gather | bytes 147456 | tf_op jit(solution)/shard_map/all_gather | solution.py:95
  25.4 12.9 %all_gather.7 = bf16[512,128]{1,0:T(8,128)(2,1)S(1)} all-gather(bf16[64,128]{1,0:T(8,128)(2,1)} %param.12), channel_id=1, replica_groups=mesh['ctx'=64,'head'=8] {'head'}, dimensions={0}, use_global_device_ids=true | all-gather | bytes 147456 | tf_op jit(solution)/shard_map/all_gather | solution.py:94
  41.2 3.8 all-to-all-start
  46.6 4.9 %all-to-all-done = bf16[64,8,176]{2,0,1:T(8,128)(2,1)S(1)} async-done(((bf16[64,8,176]{2,0,1:T(8,128)(2,1)}), bf16[64,8,176]{2,0,1:T(8,128)(2,1)S(1)}, u32[]{:S(2)}, u32[]{:S(2)}) %all-to-all-start) | async-done | bytes 180256 | tf_op jit(solution)/shard_map/all_to_all | solution.py:90
  51.5 4.5 all-to-all-start.2
  56.2 1.9 collective-permute-start.1
  58.2 2.7 collective-permute-done.1
  60.9 1.9 collective-permute-start.3
  62.8 3.6 collective-permute-done.3
  66.4 3.1 collective-permute-start.5
  69.5 5.1 %collective-permute-done.5 = bf16[16]{0:T(256)(128)(2,1)S(1)} collective-permute-done((bf16[16]{0:T(256)(128)(2,1)S(1)}, bf16[16]{0:T(256)(128)(2,1)S(1)}, u32[]{:S(2)}, u32[]{:S(2)}) %collective-permute-start.5) | collective-permute-done | bytes 64 | tf_op jit(solution)/shard_map/ppermute | solution.py:13
  74.6 1.9 collective-permute-start.7
  78.7 2.9 reshape.198
  81.7 2.5 copy.52
  84.2 159.0 %while.26 = (s32[]{:T(128)}, f32[16,512,64]{1,2,0:T(8,128)}, f32[16,128,64]{1,2,0:T(8,128)}, s32[16]{0:T(128)S(1)}, bf16[512,16,11]{0,2,1:T(8,128)(2,1)}, /*inde...) while((s32[]{:T(128)}, f32[16,512,64]{1,2,0:T(8,128)}, ...), condition=%wide.region_3.4_spmd.clone.clone, body=%wide.region_2.3_spmd.clone.sunk.clone | while | flops 44419972 | bytes 2703819 | solution.py:114
  90.8 1.7 fusion.114
  100.7 1.7 fusion.114
  110.7 1.7 fusion.114
  120.6 1.7 fusion.114
  130.5 1.7 fusion.114
  140.5 1.7 fusion.114
  150.4 1.7 fusion.114
  160.4 1.7 fusion.114
  170.3 1.7 fusion.114
  180.2 1.7 fusion.114
  190.2 1.7 fusion.114
  200.1 1.7 fusion.114
  210.1 1.7 fusion.114
  220.0 1.7 fusion.114
  229.9 1.7 fusion.114
  239.9 1.7 fusion.114
  244.3 1.9 collective-permute-start
  246.3 4.9 %collective-permute-start.9 = (bf16[16]{0:T(256)(128)(2,1)S(1)}, bf16[16]{0:T(256)(128)(2,1)S(1)}, u32[]{:S(2)}, u32[]{:S(2)}) collective-permute-start(bf16[16]{0:T(256)(128)(2,1)S(1)} %get-tuple-element.258), channel_id=1, source_target_pairs={{0,128},{8,136},{16,144},{24,152},{32,160},{40,168},{48,176},{56,1... | collective-permute-start | bytes 104 | tf_op jit(solution)/shard_map/ppermute | solution.py:13
  253.4 4.2 collective-permute-start.2
  257.6 10.5 %collective-permute-done.2 = bf16[16,128,64]{1,2,0:T(8,128)(2,1)S(1)} collective-permute-done((bf16[16,128,64]{1,2,0:T(8,128)(2,1)S(1)}, bf16[16,128,64]{1,2,0:T(8,128)(2,1)S(1)}, u32[]{:S(2)}, u32[]{:S(2)}) %collective-permute-start.2) | collective-permute-done | bytes 262176 | tf_op jit(solution)/shard_map/ppermute | solution.py:13
  268.4 6.6 %collective-permute-start.4 = (bf16[16,128,64]{1,2,0:T(8,128)(2,1)S(1)}, bf16[16,128,64]{1,2,0:T(8,128)(2,1)S(1)}, u32[]{:S(2)}, u32[]{:S(2)}) collective-permute-start(bf16[16,128,64]{1,2,0:T(8,128)(2,1)S(1)} %fusion.67), channel_id=1, source_target_pairs={{0,32},{8,40},{16,48},{24,56},{32,0},{40,8},{48,16},{56,24},{64,96... | collective-permute-start | bytes 786440 | tf_op jit(solution)/shard_map/ppermute | solution.py:13
  275.1 11.6 %collective-permute-done.4 = bf16[16,128,64]{1,2,0:T(8,128)(2,1)S(1)} collective-permute-done((bf16[16,128,64]{1,2,0:T(8,128)(2,1)S(1)}, bf16[16,128,64]{1,2,0:T(8,128)(2,1)S(1)}, u32[]{:S(2)}, u32[]{:S(2)}) %collective-permute-start.4) | collective-permute-done | bytes 262176 | tf_op jit(solution)/shard_map/ppermute | solution.py:13
  287.1 1.9 collective-permute-start.6
  289.1 5.8 %collective-permute-done.6 = bf16[16,128,64]{1,2,0:T(8,128)(2,1)S(1)} collective-permute-done((bf16[16,128,64]{1,2,0:T(8,128)(2,1)S(1)}, bf16[16,128,64]{1,2,0:T(8,128)(2,1)S(1)}, u32[]{:S(2)}, u32[]{:S(2)}) %collective-permute-start.6) | collective-permute-done | bytes 262176 | tf_op jit(solution)/shard_map/ppermute | solution.py:13
  295.1 3.1 collective-permute-start.8
  298.6 13.1 %collective-permute-done.8 = bf16[16,128,64]{1,2,0:T(8,128)(2,1)S(1)} collective-permute-done((bf16[16,128,64]{1,2,0:T(8,128)(2,1)S(1)}, bf16[16,128,64]{1,2,0:T(8,128)(2,1)S(1)}, u32[]{:S(2)}, u32[]{:S(2)}) %collective-permute-start.8) | collective-permute-done | bytes 262176 | tf_op jit(solution)/shard_map/ppermute | solution.py:13
  312.0 4.5 collective-permute-start.10
  316.9 14.3 %collective-permute-done.10 = bf16[16,128,64]{1,2,0:T(8,128)(2,1)S(1)} collective-permute-done((bf16[16,128,64]{1,2,0:T(8,128)(2,1)S(1)}, bf16[16,128,64]{1,2,0:T(8,128)(2,1)S(1)}, u32[]{:S(2)}, u32[]{:S(2)}) %collective-permute-start.10) | collective-permute-done | bytes 262176 | tf_op jit(solution)/shard_map/ppermute | solution.py:13
  332.5 111.8 %while.25 = (s32[]{:T(128)}, bf16[16,512,64]{1,2,0:T(8,128)(2,1)S(1)}, s32[16]{0:T(128)S(1)}, f32[16,512,64]{1,2,0:T(8,128)}, bf16[512,16,11]{0,2,1:T(8,128)(2,1...) while((s32[]{:T(128)}, ...), condition=%wide.region_6.7_spmd.clone, body=%wide.region_4.6_spmd.sunk.clone | while | flops 50862084 | bytes 813239 | solution.py:155
  344.9 1.6 fusion.107
  351.8 1.6 fusion.107
  446.9 17.8 %all_to_all.64 = bf16[8,64,1024]{2,1,0:T(8,128)(2,1)S(1)} all-to-all(bf16[8,64,1024]{2,1,0:T(8,128)(2,1)S(1)} %copy.58), channel_id=1, replica_groups=mesh['ctx'=64,'head'=8] {'head'}, dimensions={0} | all-to-all | bytes 2097152 | tf_op jit(solution)/shard_map/all_to_all | solution.py:157
  (409 shorter events, 194.9 us)
Async XLA Ops:
  0.0 38.6 %copy-start = (bf16[64,1408]{1,0:T(8,128)(2,1)S(1)}, bf16[64,1408]{1,0:T(8,128)(2,1)}, u32[]{:S(2)}) copy-start(bf16[64,1408]{1,0:T(8,128)(2,1)} %param.16) | copy-start | bytes 540676
  0.0 38.6 %copy-start.7 = (s32[64]{0:T(128)S(1)}, s32[64]{0:T(128)}, u32[]{:S(2)}) copy-start(s32[64]{0:T(128)} %param.15) | copy-start | bytes 772
  0.0 38.9 %copy-start.3 = (bf16[64,8192]{1,0:T(8,128)(2,1)S(1)}, bf16[64,8192]{1,0:T(8,128)(2,1)}, u32[]{:S(2)}) copy-start(bf16[64,8192]{1,0:T(8,128)(2,1)} %param.11) | copy-start | bytes 3145732
  1.6 39.5 %all-to-all-start.1 = ((bf16[8,2,512]{2,1,0:T(2,128)(2,1)}), bf16[8,2,512]{2,1,0:T(2,128)(2,1)S(1)}, u32[]{:S(2)}, u32[]{:S(2)}) async-start(bf16[8,2,512]{2,1,0:T(2,128)(2,1)} %reshape.216), calls=%async_computation.1 | async-start | bytes 32768 | tf_op jit(solution)/shard_map/all_to_all | solution.py:91
  25.4 13.0 %copy-start.4 = (bf16[512,128]{1,0:T(8,128)(2,1)}, bf16[512,128]{1,0:T(8,128)(2,1)S(1)}, u32[]{:S(2)}) copy-start(bf16[512,128]{1,0:T(8,128)(2,1)S(1)} %all_gather.6) | copy-start | bytes 393220
  41.2 10.3 %all-to-all-start = ((bf16[64,8,176]{2,0,1:T(8,128)(2,1)}), bf16[64,8,176]{2,0,1:T(8,128)(2,1)S(1)}, u32[]{:S(2)}, u32[]{:S(2)}) async-start(bf16[64,8,176]{2,0,1:T(8,128)(2,1)} %copy.44), calls=%async_computation | async-start | bytes 524288 | tf_op jit(solution)/shard_map/all_to_all | solution.py:90
  51.5 26.3 %all-to-all-start.2 = ((bf16[64,8,1024]{2,0,1:T(8,128)(2,1)}), bf16[64,8,1024]{2,0,1:T(8,128)(2,1)S(1)}, u32[]{:S(2)}, u32[]{:S(2)}) async-start(bf16[64,8,1024]{2,0,1:T(8,128)(2,1)} %bitcast.122), calls=%async_computation.2 | async-start | bytes 2097152 | tf_op jit(solution)/shard_map/all_to_all | solution.py:89
  56.2 4.6 collective-permute-start.1
  60.9 5.5 %collective-permute-start.3 = (bf16[16]{0:T(256)(128)(2,1)S(1)}, bf16[16]{0:T(256)(128)(2,1)S(1)}, u32[]{:S(2)}, u32[]{:S(2)}) collective-permute-start(bf16[16]{0:T(256)(128)(2,1)S(1)} %fusion.63), channel_id=1, source_target_pairs={{0,16},{8,24},{16,0},{24,8},{32,48},{40,56},{48,32},{56,40},{64,80... | collective-permute-start | bytes 104 | tf_op jit(solution)/shard_map/ppermute | solution.py:13
  66.4 8.2 %collective-permute-start.5 = (bf16[16]{0:T(256)(128)(2,1)S(1)}, bf16[16]{0:T(256)(128)(2,1)S(1)}, u32[]{:S(2)}, u32[]{:S(2)}) collective-permute-start(bf16[16]{0:T(256)(128)(2,1)S(1)} %convert_element_type.176), channel_id=1, source_target_pairs={{0,32},{8,40},{16,48},{24,56},{32,0},{40,8},{48,16},{56,24},{64,96... | collective-permute-start | bytes 104 | tf_op jit(solution)/shard_map/ppermute | solution.py:13
  74.6 171.7 %collective-permute-start.7 = (bf16[16]{0:T(256)(128)(2,1)S(1)}, bf16[16]{0:T(256)(128)(2,1)S(1)}, u32[]{:S(2)}, u32[]{:S(2)}) collective-permute-start(bf16[16]{0:T(256)(128)(2,1)S(1)} %convert_element_type.181), channel_id=1, source_target_pairs={{0,64},{8,72},{16,80},{24,88},{32,96},{40,104},{48,112},{56,120},{... | collective-permute-start | bytes 104 | tf_op jit(solution)/shard_map/ppermute | solution.py:13
  77.8 1.0 copy-start.2
  243.2 24.9 %copy-start.1 = (f32[16,128,64]{1,2,0:T(8,128)S(1)}, f32[16,128,64]{1,2,0:T(8,128)}, u32[]{:S(2)}) copy-start(f32[16,128,64]{1,2,0:T(8,128)} %get-tuple-element.111) | copy-start | bytes 1572868
  243.2 31.8 %copy-start.8 = (f32[128]{0:T(128)S(1)}, f32[128]{0:T(128)}, u32[]{:S(2)}) copy-start(f32[128]{0:T(128)} %param.17) | copy-start | bytes 1540
  244.3 7.8 %collective-permute-start = (bf16[16,128,64]{1,2,0:T(8,128)(2,1)S(1)}, bf16[16,128,64]{1,2,0:T(8,128)(2,1)S(1)}, u32[]{:S(2)}, u32[]{:S(2)}) collective-permute-start(bf16[16,128,64]{1,2,0:T(8,128)(2,1)S(1)} %convert_element_type.163), channel_id=1, source_target_pairs={{0,8},{8,0},{16,24},{24,16},{32,40},{40,32},{48,56},{56,48},{64,72... | collective-permute-start | bytes 786440 | tf_op jit(solution)/shard_map/ppermute | solution.py:13
  246.3 5.8 %collective-permute-start.9 = (bf16[16]{0:T(256)(128)(2,1)S(1)}, bf16[16]{0:T(256)(128)(2,1)S(1)}, u32[]{:S(2)}, u32[]{:S(2)}) collective-permute-start(bf16[16]{0:T(256)(128)(2,1)S(1)} %get-tuple-element.258), channel_id=1, source_target_pairs={{0,128},{8,136},{16,144},{24,152},{32,160},{40,168},{48,176},{56,1... | collective-permute-start | bytes 104 | tf_op jit(solution)/shard_map/ppermute | solution.py:13
  253.4 14.7 %collective-permute-start.2 = (bf16[16,128,64]{1,2,0:T(8,128)(2,1)S(1)}, bf16[16,128,64]{1,2,0:T(8,128)(2,1)S(1)}, u32[]{:S(2)}, u32[]{:S(2)}) collective-permute-start(bf16[16,128,64]{1,2,0:T(8,128)(2,1)S(1)} %fusion.68), channel_id=1, source_target_pairs={{0,16},{8,24},{16,0},{24,8},{32,48},{40,56},{48,32},{56,40},{64,80... | collective-permute-start | bytes 786440 | tf_op jit(solution)/shard_map/ppermute | solution.py:13
  268.4 18.2 %collective-permute-start.4 = (bf16[16,128,64]{1,2,0:T(8,128)(2,1)S(1)}, bf16[16,128,64]{1,2,0:T(8,128)(2,1)S(1)}, u32[]{:S(2)}, u32[]{:S(2)}) collective-permute-start(bf16[16,128,64]{1,2,0:T(8,128)(2,1)S(1)} %fusion.67), channel_id=1, source_target_pairs={{0,32},{8,40},{16,48},{24,56},{32,0},{40,8},{48,16},{56,24},{64,96... | collective-permute-start | bytes 786440 | tf_op jit(solution)/shard_map/ppermute | solution.py:13
  287.1 7.9 %collective-permute-start.6 = (bf16[16,128,64]{1,2,0:T(8,128)(2,1)S(1)}, bf16[16,128,64]{1,2,0:T(8,128)(2,1)S(1)}, u32[]{:S(2)}, u32[]{:S(2)}) collective-permute-start(bf16[16,128,64]{1,2,0:T(8,128)(2,1)S(1)} %get-tuple-element.253), channel_id=1, source_target_pairs={{0,64},{8,72},{16,80},{24,88},{32,96},{40,104},{48,112},{56,120},{... | collective-permute-start | bytes 786440 | tf_op jit(solution)/shard_map/ppermute | solution.py:13
  295.1 16.6 %collective-permute-start.8 = (bf16[16,128,64]{1,2,0:T(8,128)(2,1)S(1)}, bf16[16,128,64]{1,2,0:T(8,128)(2,1)S(1)}, u32[]{:S(2)}, u32[]{:S(2)}) collective-permute-start(bf16[16,128,64]{1,2,0:T(8,128)(2,1)S(1)} %fusion.66), channel_id=1, source_target_pairs={{0,128},{8,136},{16,144},{24,152},{32,160},{40,168},{48,176},{56,1... | collective-permute-start | bytes 786440 | tf_op jit(solution)/shard_map/ppermute | solution.py:13
  298.6 33.9 %copy-start.5 = (bf16[512,128]{1,0:T(8,128)(2,1)S(1)}, bf16[512,128]{1,0:T(8,128)(2,1)}, u32[]{:S(2)}) copy-start(bf16[512,128]{1,0:T(8,128)(2,1)} %copy-done.4) | copy-start | bytes 393220
  312.0 19.1 %collective-permute-start.10 = (bf16[16,128,64]{1,2,0:T(8,128)(2,1)S(1)}, bf16[16,128,64]{1,2,0:T(8,128)(2,1)S(1)}, u32[]{:S(2)}, u32[]{:S(2)}) collective-permute-start(bf16[16,128,64]{1,2,0:T(8,128)(2,1)S(1)} %fusion.42), channel_id=1, source_target_pairs={{0,256},{8,264},{16,272},{24,280},{32,288},{40,296},{48,304},{56,3... | collective-permute-start | bytes 786440 | tf_op jit(solution)/shard_map/ppermute | solution.py:13
  331.4 1.2 copy-start.6
where the time goes:
time: 472 us; the launch traced here: 466 us
  local copies, waits for them, and re-layouts  95.3 us (20%)
  matrix products  75.6 us (16%)
  waiting for transfers between devices  72.5 us (15%)
  loops' own time  64.2 us (14%)
  other arithmetic  59 us (12%)
  starting transfers between devices  54.4 us (12%)
  blocking collectives  44.4 us (9%)
    ppermute x11, waiting for transfers between devices, swapped(): lax.ppermute(x, axis, [(i, i ^ 1 << apart) for i in range(lax.axis_size(a...  67.5 us
    ppermute x11, starting transfers between devices, swapped(): lax.ppermute(x, axis, [(i, i ^ 1 << apart) for i in range(lax.axis_size(a...  36 us
    another operation x1, loops' own time, on_device(): mixed_rows = lax.map(second_pass, jnp.arange(local_heads))  33.8 us
    another operation x1, loops' own time, on_device(): local_all, states = lax.map(first_pass, jnp.arange(local_heads))  30.4 us
    dot_general x16, matrix products, head_local(): return jnp.dot(weight, head_input, preferred_element_type=jnp.float32)  27.3 us
    dynamic_update_slice x16, other arithmetic, on_device(): mixed_rows = lax.map(second_pass, jnp.arange(local_heads))  26 us
    dot_general x16, matrix products, head_state(): jnp.einsum('tn,tp->np', state_in, carried.astype(jnp.bfloat16), preferred...  25.6 us
    dynamic_slice x32, local copies, waits for them, and re-layouts, on_device(): local_all, states = lax.map(first_pass, jnp.arange(local_heads))  20.8 us
  transfers between devices with their start and end apart: 14, of which 10 were waited for; matrix products, arithmetic and copies ran while one was open for 30% of the time, Pallas kernels for 0%

commit v1 on v0

v1 whole, which is shorter than its diff:
```python
import functools

import jax
import jax.numpy as jnp
from jax import lax
from jax.experimental import pallas as pl
from jax.experimental.pallas import tpu as pltpu
from jax.sharding import PartitionSpec as P

HEADS = 128
HEAD_DIM = 64
STATE = 128
SPAN = 64
LEVELS = 11
CODES = 64
NY = 8
LANES = 128
MESH = pl.DeviceIdType.MESH
F32 = jnp.float32
BF16 = jnp.bfloat16


def bits_of(n):
    return n.bit_length() - 1


def dot(a, b):
    return jnp.dot(a, b, preferred_element_type=F32)


def dot_t(a, b):
    return lax.dot_general(a, b, (((0,), (0,)), ((), ())), preferred_element_type=F32)


def iota(shape, dim):
    return lax.broadcasted_iota(jnp.int32, shape, dim)


def spread(v, first):
    idx = first + (iota(v.shape, 1) >> 6)
    return jnp.take_along_axis(v, idx, axis=1, mode="promise_in_bounds")


def kernel(
    nh, ny, nz,
    x, b, c, d, codes, tab, skip, out,
    xc, xr, br, cr, aux, auxr, o0, rows, te, oh, we, sg, lbs, li,
    sb, r1, pb, tz, r2, yb, zb, bks, tau, lt, pg, io, ir,
    xs, bs, cs, axs, taus, lts, r1s, l0s, ys, r2s, ags, ios,
):
    hl = HEADS // nh
    groups = hl // 2
    gp = groups // ny
    hbits, ybits, zbits = bits_of(nh), bits_of(ny), bits_of(nz)
    nlev = hbits + ybits + zbits
    hd = lax.axis_index("head")
    k = lax.axis_index("ctx")
    y = lax.rem(k, ny)
    z = lax.div(k, ny)

    def to_head(j):
        return {"head": j}

    def to_y(j):
        return {"ctx": z * ny + j}

    def to_z(j):
        return {"ctx": j * ny + y}

    def remote(src, dst, send, recv, where):
        return pltpu.make_async_remote_copy(
            src_ref=src, dst_ref=dst, send_sem=send, recv_sem=recv,
            device_id=where, device_id_type=MESH,
        )

    heads_round = [lax.rem(hd + i, nh) for i in range(1, nh)]
    y_round = [lax.rem(y + i, ny) for i in range(1, ny)]
    z_round = [lax.rem(z + i, nz) for i in range(1, nz)]

    lt[...] = jnp.zeros_like(lt)
    barrier = pltpu.get_barrier_semaphore()
    for j in heads_round:
        pl.semaphore_signal(barrier, inc=1, device_id=to_head(j), device_id_type=MESH)
    for j in y_round:
        pl.semaphore_signal(barrier, inc=1, device_id=to_y(j), device_id_type=MESH)
    for j in z_round:
        pl.semaphore_signal(barrier, inc=1, device_id=to_z(j), device_id_type=MESH)

    lower = iota((SPAN, SPAN), 0) >= iota((SPAN, SPAN), 1)
    run = dot(jnp.where(lower, 1.0, 0.0).astype(BF16), d[...])
    tot = run[SPAN - 1:SPAN, :]
    fac = jnp.exp(tot - run)

    pairs = HEADS // 2
    first = 2 * iota((pairs, LANES), 0) + (iota((pairs, LANES), 1) >> 6)
    tot_pairs = jnp.take_along_axis(
        jnp.broadcast_to(tot, (pairs, LANES)), first, axis=1, mode="promise_in_bounds"
    )
    code_row = codes[...].astype(F32)
    for j in range(nh):
        aux[j, 0:groups, :] = tot_pairs[j * groups:(j + 1) * groups, :]
        aux[j, groups:groups + 8, 0:SPAN] = jnp.broadcast_to(code_row, (8, SPAN))
        aux[j, groups:groups + 8, SPAN:] = jnp.zeros((8, LANES - SPAN), F32)
    auxr[hd] = aux[hd]
    br[hd] = b[...]
    cr[hd] = c[...]

    def carry(j):
        def one(p, _):
            cols = pl.ds(pl.multiple_of(p * LANES, LANES), LANES)
            src = pl.ds(pl.multiple_of((j * groups + p) * LANES, LANES), LANES)
            m = spread(fac, 2 * (j * groups + p))
            xc[j, :, cols] = (m * x[:, src].astype(F32)).astype(BF16)
            return 0

        lax.fori_loop(0, groups, one, 0, unroll=4)

    def send_x(j):
        return remote(xc.at[j], xr.at[hd], xs.at[0, j], xs.at[1, hd], to_head(j))

    def send_b(j):
        return remote(b, br.at[hd], bs.at[0, j], bs.at[1, hd], to_head(j))

    def send_c(j):
        return remote(c, cr.at[hd], cs.at[0, j], cs.at[1, hd], to_head(j))

    def send_a(j):
        return remote(aux.at[j], auxr.at[hd], axs.at[0, j], axs.at[1, hd], to_head(j))

    def send_o(j):
        return remote(io.at[j], ir.at[hd], ios.at[0, j], ios.at[1, hd], to_head(j))

    carry(heads_round[0])
    pl.semaphore_wait(barrier, (nh - 1) + (ny - 1) + (nz - 1))
    for j in heads_round:
        send_a(j).start()
    for j in heads_round:
        send_b(j).start()
    for i, j in enumerate(heads_round):
        if i:
            carry(j)
        send_x(j).start()
    for j in heads_round:
        send_c(j).start()
    carry(hd)
    xr[hd] = xc[hd]

    def recv_a(j):
        return remote(aux.at[j], auxr.at[j], axs.at[0, j], axs.at[1, j], to_head(j))

    for j in heads_round:
        recv_a(j).wait_recv()
    mine = auxr[0, 0:groups, :]
    for g in range(nh):
        pg[g] = jnp.exp(mine) if g else jnp.ones((groups, LANES), F32)
        if g:
            mine = mine + auxr[g, 0:groups, :]
    tau[y] = mine

    def send_tau(j):
        return remote(tau.at[y], tau.at[y], taus.at[0, j], taus.at[1, y], to_y(j))

    def recv_tau(j):
        return remote(tau.at[j], tau.at[j], taus.at[0, j], taus.at[1, j], to_y(j))

    for j in y_round:
        send_tau(j).start()

    cols0 = iota((LEVELS * HEADS, LANES), 0)
    lane0 = iota((LEVELS * HEADS, LANES), 1)
    tab0 = dot(tab[...], jnp.where(cols0 == lane0 * LEVELS, 1.0, 0.0).astype(BF16)).astype(BF16)
    code_t = jnp.where(
        jnp.broadcast_to(code_row, (CODES, SPAN)) == iota((CODES, SPAN), 0).astype(F32), 1.0, 0.0
    ).astype(BF16)
    w0 = dot_t(code_t, tab0)
    rows[0] = w0 * jnp.exp(run - tot)
    rows[1] = jnp.exp(run)

    per = LANES // hl
    for t in range(-(-nlev // per)):
        lev = 1 + t * per + lane0 // hl
        want = (hd * hl + lax.rem(lane0, hl)) * LEVELS + lev
        picked = dot(tab[...], jnp.where(cols0 == want, 1.0, 0.0).astype(BF16))
        for l in range(t * per, min(nlev, (t + 1) * per)):
            for p in range(groups):
                te[l, :, p * LANES:(p + 1) * LANES] = spread(
                    picked, (l - t * per) * hl + 2 * p
                ).astype(BF16)
    eye = jnp.where(iota((CODES, CODES), 0) == iota((CODES, CODES), 1), 1.0, 0.0).astype(BF16)
    for g in range(nh):
        row = auxr[g, groups:groups + 1, 0:SPAN]
        hot = jnp.where(
            jnp.broadcast_to(row, (CODES, SPAN)) == iota((CODES, SPAN), 0).astype(F32), 1.0, 0.0
        ).astype(BF16)
        oh[g * SPAN:(g + 1) * SPAN, :] = dot_t(hot, eye).astype(BF16)

    scores = lax.dot_general(
        c[...], b[...], (((1,), (1,)), ((), ())), preferred_element_type=F32
    )
    near = jnp.where(lower, scores, 0.0).astype(BF16)
    gain = jnp.broadcast_to(skip[...], (SPAN, LANES))

    def level0(j, _):
        v = dot(near, xc[j])
        for p in range(groups):
            cols = pl.ds(pl.multiple_of((j * groups + p) * LANES, LANES), LANES)
            at = 2 * (j * groups + p)
            o0[:, cols] = (
                spread(rows[0], at) * v[:, p * LANES:(p + 1) * LANES]
                + spread(gain, at) * x[:, cols].astype(F32)
            )
        return 0

    lax.fori_loop(0, nh, level0, 0)

    for j in y_round:
        recv_tau(j).wait_recv()
    line = tau[0]
    for j in range(1, ny):
        line = line + tau[j]
    lt[z] = line

    def send_lt(i):
        return remote(lt.at[z], lt.at[z], lts.at[0, z + i], lts.at[1, z], to_z(z + i))

    def recv_lt(i):
        return remote(lt.at[z], lt.at[z - i], lts.at[0, z], lts.at[1, z - i], to_z(z - i))

    for i in range(1, nz):
        @pl.when(z + i < nz)
        def _():
            send_lt(i).start()

    def recv_x(j):
        return remote(xc.at[j], xr.at[j], xs.at[0, j], xs.at[1, j], to_head(j))

    def recv_b(j):
        return remote(b, br.at[j], bs.at[0, j], bs.at[1, j], to_head(j))

    sg[hd] = dot_t(br[hd], xr[hd])
    for j in heads_round:
        recv_b(j).wait_recv()
    for j in heads_round:
        recv_x(j).wait_recv()
        sg[j] = dot_t(br[j], xr[j])

    offs = [0]
    for m in range(hbits):
        offs.append(offs[-1] + (nh >> (m + 1)))

    def fold(p, _):
        cols = pl.ds(pl.multiple_of(p * LANES, LANES), LANES)
        cur = [sg[g, :, cols] for g in range(nh)]
        dec = [auxr[g, pl.ds(p, 1), :] for g in range(nh)]
        for m in range(hbits):
            new, new_dec = [], []
            for i in range(len(cur) // 2):
                lbs[offs[m] + i, :, cols] = cur[2 * i].astype(BF16)
                new.append(cur[2 * i] * jnp.exp(dec[2 * i + 1]) + cur[2 * i + 1])
                new_dec.append(dec[2 * i] + dec[2 * i + 1])
            cur, dec = new, new_dec
        sb[p] = cur[0].astype(BF16)
        return 0

    lax.fori_loop(0, groups, fold, 0)

    def send_r1(j):
        return remote(
            sb.at[pl.ds(j * gp, gp)], r1.at[y], r1s.at[0, j], r1s.at[1, y], to_y(j)
        )

    def recv_r1(j):
        return remote(sb.at[pl.ds(j * gp, gp)], r1.at[j], r1s.at[0, j], r1s.at[1, j], to_y(j))

    for j in y_round:
        send_r1(j).start()

    def send_l0():
        return remote(sb, yb.at[0], l0s.at[0], l0s.at[1], to_y(y + 1))

    def recv_l0():
        return remote(sb, yb.at[0], l0s.at[0], l0s.at[1], to_y(y - 1))

    @pl.when(lax.rem(y, 2) == 0)
    def _():
        send_l0().start()

    for q in range(gp):
        r1[y, q] = sb[y * gp + q]

    for l in range(nlev):
        for g in range(0, nh, 2):
            w = dot(oh[g * SPAN:(g + 2) * SPAN, :], te[l]).astype(BF16)
            we[l, g] = w[0:SPAN]
            we[l, g + 1] = w[SPAN:]

    for i in range(1, nz):
        @pl.when(z - i >= 0)
        def _():
            recv_lt(i).wait_recv()
    for j in y_round:
        recv_r1(j).wait_recv()

    yoffs = [0]
    for m in range(1, ybits):
        yoffs.append(yoffs[-1] + (ny >> (m + 1)))
    for q in range(gp):
        cur = [r1[j, q].astype(F32) for j in range(ny)]
        dec = [tau[j, pl.ds(y * gp + q, 1), :] for j in range(ny)]
        for m in range(ybits):
            new, new_dec = [], []
            for i in range(len(cur) // 2):
                if m:
                    pb[yoffs[m - 1] + i, q] = cur[2 * i].astype(BF16)
                new.append(cur[2 * i] * jnp.exp(dec[2 * i + 1]) + cur[2 * i + 1])
                new_dec.append(dec[2 * i] + dec[2 * i + 1])
            cur, dec = new, new_dec
        r2[z, q] = cur[0].astype(BF16)
        tz[q] = cur[0].astype(BF16)

    def send_r2(i):
        return remote(tz, r2.at[z], r2s.at[0, z + i], r2s.at[1, z], to_z(z + i))

    def recv_r2(i):
        return remote(tz, r2.at[z - i], r2s.at[0, z], r2s.at[1, z - i], to_z(z - i))

    for i in range(1, nz):
        @pl.when(z + i < nz)
        def _():
            send_r2(i).start()

    def bit(v, m):
        return lax.rem(lax.div(v, 1 << m), 2) == 1

    def send_yb(m, j):
        return remote(
            pb.at[yoffs[m - 1] + lax.div(j, 2 << m)], yb.at[m, pl.ds(y * gp, gp)],
            ys.at[0, m, j], ys.at[1, m, y], to_y(j),
        )

    def recv_yb(m, j):
        return remote(
            pb.at[0], yb.at[m, pl.ds(j * gp, gp)], ys.at[0, m, j], ys.at[1, m, j], to_y(j)
        )

    for m in range(1, ybits):
        for j in y_round:
            @pl.when(bit(j, m))
            def _():
                send_yb(m, j).start()

        @pl.when(bit(y, m))
        def _():
            for q in range(gp):
                yb[m, y * gp + q] = pb[yoffs[m - 1] + lax.div(y, 2 << m), q]

    def recv_c(j):
        return remote(c, cr.at[j], cs.at[0, j], cs.at[1, j], to_head(j))

    for j in heads_round:
        recv_c(j).wait_recv()
    for g in range(nh):
        acc = [None] * groups
        for m in range(hbits):
            if not g >> m & 1:
                continue
            v = dot(cr[g], lbs[offs[m] + (g >> (m + 1))])
            gap = None
            for before in range(g >> m << m, g):
                row = auxr[before, 0:groups, :]
                gap = row if gap is None else gap + row
            scale = None if gap is None else jnp.exp(gap)
            for p in range(groups):
                cols = slice(p * LANES, (p + 1) * LANES)
                term = we[m, g, :, cols].astype(F32) * v[:, cols]
                if scale is not None:
                    term = term * scale[p:p + 1, :]
                acc[p] = term if acc[p] is None else acc[p] + term
        for p in range(groups):
            cols = slice(p * LANES, (p + 1) * LANES)
            li[g, :, cols] = jnp.zeros((SPAN, LANES), F32) if acc[p] is None else acc[p]

    for i in range(1, nz):
        @pl.when(z - i >= 0)
        def _():
            recv_r2(i).wait_recv()
    for m in range(zbits):
        @pl.when(bit(z, m))
        def _():
            base = lax.div(z, 1 << m) * (1 << m)
            for q in range(gp):
                row = pl.ds(y * gp + q, 1)
                acc = r2[base - 1, q].astype(F32)
                gap = lt[base - 1, row, :]
                for i in range(2, (1 << m) + 1):
                    acc = acc + r2[base - i, q].astype(F32) * jnp.exp(gap)
                    gap = gap + lt[base - i, row, :]
                zb[m, y * gp + q] = acc.astype(BF16)

    right, left = lax.rem(y + 1, ny), lax.rem(y + ny - 1, ny)
    right_steps = ny // 2
    left_steps = ny - 1 - right_steps

    def hop(m, way, s):
        if way == 0:
            own = lax.rem(y + ny - s, ny)
            goal = right
        else:
            own = lax.rem(y + s, ny)
            goal = left
        part = zb.at[m, pl.ds(own * gp, gp)]
        return remote(part, part, ags.at[0, m, way, s], ags.at[1, m, way, s], to_y(goal))

    def landed(m, way, s):
        own = lax.rem(y + ny - s - 1, ny) if way == 0 else lax.rem(y + s + 1, ny)
        part = zb.at[m, pl.ds(own * gp, gp)]
        return remote(
            part, part, ags.at[0, m, way, s], ags.at[1, m, way, s], to_y(left if way == 0 else right)
        )

    for s in range(right_steps):
        for m in range(zbits):
            @pl.when(bit(z, m))
            def _():
                for way in range(2):
                    if s < (right_steps, left_steps)[way]:
                        if s:
                            landed(m, way, s - 1).wait_recv()
                        hop(m, way, s).start()

    def before_y(lo):
        gap = jnp.zeros((groups, LANES), F32)
        for j in range(ny):
            gap = gap + jnp.where(jnp.logical_and(j >= lo, j < y), tau[j], 0.0)
        return gap

    def before_z(lo):
        gap = jnp.zeros((groups, LANES), F32)
        for j in range(nz):
            gap = gap + jnp.where(jnp.logical_and(j >= lo, j < z), lt[j], 0.0)
        return gap

    def put(slot, part, gap):
        scale = jnp.exp(gap)
        for p in range(groups):
            bks[slot, :, p * LANES:(p + 1) * LANES] = (
                part[p].astype(F32) * scale[p:p + 1, :]
            ).astype(BF16)

    for m in range(ybits):
        @pl.when(bit(y, m))
        def _():
            if m == 0:
                recv_l0().wait_recv()
            else:
                for j in y_round:
                    recv_yb(m, j).wait_recv()
            put(m, yb.at[m], before_y(lax.div(y, 1 << m) * (1 << m)))

        @pl.when(jnp.logical_not(bit(y, m)))
        def _():
            bks[m] = jnp.zeros((STATE, hl * HEAD_DIM), BF16)

    for m in range(zbits):
        @pl.when(bit(z, m))
        def _():
            for way in range(2):
                last = (right_steps, left_steps)[way] - 1
                if last >= 0:
                    landed(m, way, last).wait_recv()
            put(
                ybits + m, zb.at[m],
                before_y(0) + before_z(lax.div(z, 1 << m) * (1 << m)),
            )

        @pl.when(jnp.logical_not(bit(z, m)))
        def _():
            bks[ybits + m] = jnp.zeros((STATE, hl * HEAD_DIM), BF16)

    def cross(g):
        acc = [None] * groups
        for m in range(ybits + zbits):
            v = dot(cr[g], bks[m])
            for p in range(groups):
                cols = slice(p * LANES, (p + 1) * LANES)
                term = we[hbits + m, g, :, cols].astype(F32) * v[:, cols]
                acc[p] = term if acc[p] is None else acc[p] + term
        scale = pg[g]
        for p in range(groups):
            cols = slice(p * LANES, (p + 1) * LANES)
            io[g, :, cols] = (acc[p] * scale[p:p + 1, :] + li[g, :, cols]).astype(BF16)

    for j in heads_round:
        cross(j)
        send_o(j).start()
    cross(hd)
    ir[hd] = io[hd]

    def recv_o(j):
        return remote(io.at[j], ir.at[j], ios.at[0, j], ios.at[1, j], to_head(j))

    def finish(j):
        def one(p, _):
            cols = pl.ds(pl.multiple_of((j * groups + p) * LANES, LANES), LANES)
            part = pl.ds(pl.multiple_of(p * LANES, LANES), LANES)
            m = spread(rows[1], 2 * (j * groups + p))
            out[:, cols] = (o0[:, cols] + m * ir[j, :, part].astype(F32)).astype(BF16)
            return 0

        lax.fori_loop(0, groups, one, 0, unroll=4)

    finish(hd)
    for i in range(nh - 2, -1, -1):
        j = heads_round[i]
        recv_o(j).wait_recv()
        finish(j)

    for j in heads_round:
        send_a(j).wait_send()
        send_b(j).wait_send()
        send_x(j).wait_send()
        send_c(j).wait_send()
        send_o(j).wait_send()
    for j in y_round:
        send_tau(j).wait_send()
        send_r1(j).wait_send()
        for m in range(1, ybits):
            @pl.when(bit(j, m))
            def _():
                send_yb(m, j).wait_send()

    @pl.when(lax.rem(y, 2) == 0)
    def _():
        send_l0().wait_send()

    for i in range(1, nz):
        @pl.when(z + i < nz)
        def _():
            send_lt(i).wait_send()
            send_r2(i).wait_send()
    for s in range(right_steps):
        for m in range(zbits):
            @pl.when(bit(z, m))
            def _():
                for way in range(2):
                    if s < (right_steps, left_steps)[way]:
                        hop(m, way, s).wait_send()


def on_device(nh, ny, nz, token_inputs, state_in, state_out, log_decay, token_codes, table, gain):
    hl = HEADS // nh
    groups = hl // 2
    gp = groups // ny
    wide = hl * HEAD_DIM
    hbits, ybits, zbits = bits_of(nh), bits_of(ny), bits_of(nz)
    nlev = hbits + ybits + zbits
    vm = pltpu.VMEM
    sem = pltpu.SemaphoreType.DMA
    pieces = sum(ny >> (m + 1) for m in range(1, ybits))
    return pl.pallas_call(
        functools.partial(kernel, nh, ny, nz),
        out_shape=jax.ShapeDtypeStruct((SPAN, HEADS * HEAD_DIM), BF16),
        in_specs=[pl.BlockSpec(memory_space=pltpu.VMEM)] * 7,
        out_specs=pl.BlockSpec(memory_space=pltpu.VMEM),
        scratch_shapes=[
            vm((nh, SPAN, wide), BF16),
            vm((nh, SPAN, wide), BF16),
            vm((nh, SPAN, STATE), BF16),
            vm((nh, SPAN, STATE), BF16),
            vm((nh, groups + 8, LANES), F32),
            vm((nh, groups + 8, LANES), F32),
            vm((SPAN, HEADS * HEAD_DIM), F32),
            vm((2, SPAN, LANES), F32),
            vm((nlev, CODES, wide), BF16),
            vm((nh * SPAN, CODES), BF16),
            vm((nlev, nh, SPAN, wide), BF16),
            vm((nh, STATE, wide), F32),
            vm((nh - 1, STATE, wide), BF16),
            vm((nh, SPAN, wide), F32),
            vm((groups, STATE, LANES), BF16),
            vm((ny, gp, STATE, LANES), BF16),
            vm((max(pieces, 1), gp, STATE, LANES), BF16),
            vm((gp, STATE, LANES), BF16),
            vm((nz, gp, STATE, LANES), BF16),
            vm((ybits, groups, STATE, LANES), BF16),
            vm((max(zbits, 1), groups, STATE, LANES), BF16),
            vm((ybits + zbits, STATE, wide), BF16),
            vm((ny, groups, LANES), F32),
            vm((nz, groups, LANES), F32),
            vm((nh, groups, LANES), F32),
            vm((nh, SPAN, wide), BF16),
            vm((nh, SPAN, wide), BF16),
            sem((2, nh)),
            sem((2, nh)),
            sem((2, nh)),
            sem((2, nh)),
            sem((2, ny)),
            sem((2, nz)),
            sem((2, ny)),
            sem((2,)),
            sem((2, max(ybits, 1), ny)),
            sem((2, nz)),
            sem((2, max(zbits, 1), 2, max(ny // 2, 1))),
            sem((2, nh)),
        ],
        compiler_params=pltpu.CompilerParams(
            collective_id=0, has_side_effects=True, vmem_limit_bytes=60 << 20
        ),
    )(
        token_inputs, state_in, state_out, log_decay,
        token_codes.reshape(1, SPAN), table, gain.reshape(1, HEADS),
    )


def solution(mesh, ny=NY):
    nh = mesh.shape["head"]
    nz = mesh.shape["ctx"] // ny
    return jax.shard_map(
        functools.partial(on_device, nh, ny, nz),
        mesh=mesh,
        in_specs=(
            P(("ctx", "head"), None),
            P(("ctx", "head"), None),
            P(("ctx", "head"), None),
            P(("ctx", "head"), None),
            P(("ctx", "head")),
            P(),
            P(),
        ),
        out_specs=P(("ctx", "head"), None),
        check_vma=False,
    )
```

time: 472 us -> 80.5 us (0.17)
  the two profiles are of different devices: /device:TPU:1 before, /device:TPU:65 now
where the time goes in v1:
time: 80.5 us; the launch traced here: 80.3 us
  Pallas kernels  78.1 us (97%)
  local copies, waits for them, and re-layouts  2.26 us (3%)
    pallas_call x1, Pallas kernels, on_device(): pl.pallas_call(functools.partial(kernel, nh, ny, nz), out_shape=jax.Shape...  78.1 us
    unnamed x1, local copies, waits for them, and re-layouts  2.26 us

profile of v1, /device:TPU:65, one launch (start us, length us, event | category | flops | bytes accessed | tf_op | source)
XLA Modules:
  0.0 80.3 jit_solution(11734115564909224272)
XLA Ops:
  0.0 78.1 %shard_map.73 = bf16[64,8192]{1,0:T(8,128)(2,1)} custom-call(bf16[64,8192]{1,0:T(8,128)(2,1)} %x.1, bf16[64,128]{1,0:T(8,128)(2,1)} %b.1, bf16[64,128]{1,0:T(8,128)(2,1)} %c.1, bf16[64,128]{1,0:T(8,128)(2,1)} %d.1, s32[1,64]{1,0:T(1,128)} %bitcast.2, bf16[64,1408]{1,0:T(8,128)(2,1)} %tab.1, f32[1,128]{1,0:T(1,128)} %bitcast.3), custom_call_target="tpu_custom_call" | custom-call | tf_op jit(solution)/shard_map/pallas_call | solution.py:560
  78.1 2.3 %copy.9 = bf16[64,8192]{1,0:T(8,128)(2,1)} copy(bf16[64,8192]{1,0:T(8,128)(2,1)} %shard_map.73) | data formatting | bytes 2097152

commit v2 on v1

v2 whole, which is shorter than its diff:
```python
import functools

import jax
import jax.numpy as jnp
from jax import lax
from jax.experimental import pallas as pl
from jax.experimental.pallas import tpu as pltpu
from jax.sharding import PartitionSpec as P

HEADS = 128
HEAD_DIM = 64
STATE = 128
SPAN = 64
LEVELS = 11
CODES = 64
NY = 8
LANES = 128
CHUNKS = 2
SPLIT = 2
TILE = 256
VMEM_LIMIT = 44 << 20
MESH = pl.DeviceIdType.MESH
F32 = jnp.float32
BF16 = jnp.bfloat16


def bits_of(n):
    return n.bit_length() - 1


def dot(a, b):
    return jnp.dot(a, b, preferred_element_type=F32)


def dot_t(a, b):
    return lax.dot_general(a, b, (((0,), (0,)), ((), ())), preferred_element_type=F32)


def iota(shape, dim):
    return lax.broadcasted_iota(jnp.int32, shape, dim)


def spread(v, first):
    idx = first + (iota(v.shape, 1) >> 6)
    return jnp.take_along_axis(v, idx, axis=1, mode="promise_in_bounds")


def kernel(
    nh, ny, nz,
    x, b, c, d, codes, tab, skip, out,
    xc, xr, br, cr, aux, auxr, o0, er, rows, te, oh, we, sg, lbs, li,
    sb, r1, pb, tz, r2, yb, zb, bks, tau, lt, pg, io, ir,
    xs, bs, cs, axs, taus, lts, r1s, l0s, ys, r2s, ags, ios,
):
    hl = HEADS // nh
    groups = hl // 2
    gc = groups // CHUNKS
    units = gc * SPLIT
    up = units // ny
    rp = STATE // SPLIT
    wc = gc * LANES
    tiles = [slice(i, i + TILE) for i in range(0, wc, TILE)]
    hbits, ybits, zbits = bits_of(nh), bits_of(ny), bits_of(nz)
    nlev = hbits + ybits + zbits
    chunks = range(CHUNKS)
    hd = lax.axis_index("head")
    k = lax.axis_index("ctx")
    y = lax.rem(k, ny)
    z = lax.div(k, ny)
    chip, core = lax.div(hd, 2), lax.rem(hd, 2)

    def to_head(j):
        return {"head": j}

    def to_y(j):
        return {"ctx": z * ny + j}

    def to_z(j):
        return {"ctx": j * ny + y}

    def remote(src, dst, send, recv, where):
        return pltpu.make_async_remote_copy(
            src_ref=src, dst_ref=dst, send_sem=send, recv_sem=recv,
            device_id=where, device_id_type=MESH,
        )

    def bit(v, m):
        return lax.rem(lax.div(v, 1 << m), 2) == 1

    hops = sorted(range(1, nh // 2), key=lambda o: -min(o, nh // 2 - o))
    chips_round = [lax.rem(chip + o, nh // 2) for o in hops]
    heads_round = []
    for q in chips_round:
        heads_round += [2 * q + core, 2 * q + 1 - core]
    heads_round.append(2 * chip + 1 - core)
    y_round = [lax.rem(y + i, ny) for i in range(1, ny)]
    z_round = [lax.rem(z + i, nz) for i in range(1, nz)]

    lt[...] = jnp.zeros_like(lt)
    barrier = pltpu.get_barrier_semaphore()
    for j in heads_round:
        pl.semaphore_signal(barrier, inc=1, device_id=to_head(j), device_id_type=MESH)
    for j in y_round:
        pl.semaphore_signal(barrier, inc=1, device_id=to_y(j), device_id_type=MESH)
    for j in z_round:
        pl.semaphore_signal(barrier, inc=1, device_id=to_z(j), device_id_type=MESH)

    lower = iota((SPAN, SPAN), 0) >= iota((SPAN, SPAN), 1)
    run = dot(jnp.where(lower, 1.0, 0.0).astype(BF16), d[...])
    tot = run[SPAN - 1:SPAN, :]
    fac = jnp.exp(tot - run)

    pairs = HEADS // 2
    first = 2 * iota((pairs, LANES), 0) + (iota((pairs, LANES), 1) >> 6)
    tot_pairs = jnp.take_along_axis(
        jnp.broadcast_to(tot, (pairs, LANES)), first, axis=1, mode="promise_in_bounds"
    )
    code_row = codes[...].astype(F32)
    for j in range(nh):
        aux[j, 0:groups, :] = tot_pairs[j * groups:(j + 1) * groups, :]
        aux[j, groups:groups + 8, 0:SPAN] = jnp.broadcast_to(code_row, (8, SPAN))
        aux[j, groups:groups + 8, SPAN:] = jnp.zeros((8, LANES - SPAN), F32)
    auxr[hd] = aux[hd]
    br[hd] = b[...]
    cr[hd] = c[...]

    def carry(ch, j):
        def one(p, _):
            cols = pl.ds(pl.multiple_of(p * LANES, LANES), LANES)
            at = j * groups + ch * gc + p
            src = pl.ds(pl.multiple_of(at * LANES, LANES), LANES)
            m = spread(fac, 2 * at)
            xc[ch, j, :, cols] = (m * x[:, src].astype(F32)).astype(BF16)
            return 0

        lax.fori_loop(0, gc, one, 0, unroll=4)

    def move_x(ch, j, src):
        return remote(
            xc.at[ch, j], xr.at[ch, src], xs.at[0, ch, j], xs.at[1, ch, src], to_head(j)
        )

    def move_b(j, src):
        return remote(b, br.at[src], bs.at[0, j], bs.at[1, src], to_head(j))

    def move_c(j, src):
        return remote(c, cr.at[src], cs.at[0, j], cs.at[1, src], to_head(j))

    def move_a(j, src):
        return remote(aux.at[j], auxr.at[src], axs.at[0, j], axs.at[1, src], to_head(j))

    def move_o(ch, j, src):
        return remote(
            io.at[ch, j], ir.at[ch, src], ios.at[0, ch, j], ios.at[1, ch, src], to_head(j)
        )

    carry(0, heads_round[0])
    pl.semaphore_wait(barrier, (nh - 1) + (ny - 1) + (nz - 1))
    for j in heads_round:
        move_a(j, hd).start()
    for j in heads_round:
        move_b(j, hd).start()
    for ch in chunks:
        for i, j in enumerate(heads_round):
            if i or ch:
                carry(ch, j)
            move_x(ch, j, hd).start()
    for ch in chunks:
        carry(ch, hd)
        xr[ch, hd] = xc[ch, hd]

    for j in heads_round:
        move_a(j, j).wait_recv()
    mine = auxr[0, 0:groups, :]
    for g in range(nh):
        pg[g] = jnp.exp(mine) if g else jnp.ones((groups, LANES), F32)
        if g:
            mine = mine + auxr[g, 0:groups, :]
    tau[y] = mine

    def move_tau(j, src):
        return remote(tau.at[y], tau.at[src], taus.at[0, j], taus.at[1, src], to_y(j))

    for j in y_round:
        move_tau(j, y).start()

    cols0 = iota((LEVELS * HEADS, LANES), 0)
    lane0 = iota((LEVELS * HEADS, LANES), 1)
    tab0 = dot(tab[...], jnp.where(cols0 == lane0 * LEVELS, 1.0, 0.0).astype(BF16)).astype(BF16)
    code_t = jnp.where(
        jnp.broadcast_to(code_row, (CODES, SPAN)) == iota((CODES, SPAN), 0).astype(F32), 1.0, 0.0
    ).astype(BF16)
    w0 = dot_t(code_t, tab0)
    rows[0] = w0 * jnp.exp(run - tot)
    rows[1] = jnp.exp(run)

    per = LANES // hl
    for t in range(-(-nlev // per)):
        lev = 1 + t * per + lane0 // hl
        want = (hd * hl + lax.rem(lane0, hl)) * LEVELS + lev
        picked = dot(tab[...], jnp.where(cols0 == want, 1.0, 0.0).astype(BF16))
        for l in range(t * per, min(nlev, (t + 1) * per)):
            for p in range(groups):
                te[l, :, p * LANES:(p + 1) * LANES] = spread(
                    picked, (l - t * per) * hl + 2 * p
                ).astype(BF16)
    eye = jnp.where(iota((CODES, CODES), 0) == iota((CODES, CODES), 1), 1.0, 0.0).astype(BF16)
    for g in range(nh):
        row = auxr[g, groups:groups + 1, 0:SPAN]
        hot = jnp.where(
            jnp.broadcast_to(row, (CODES, SPAN)) == iota((CODES, SPAN), 0).astype(F32), 1.0, 0.0
        ).astype(BF16)
        oh[g * SPAN:(g + 1) * SPAN, :] = dot_t(hot, eye).astype(BF16)

    scores = lax.dot_general(
        c[...], b[...], (((1,), (1,)), ((), ())), preferred_element_type=F32
    )
    near = jnp.where(lower, scores, 0.0).astype(BF16)
    gain = jnp.broadcast_to(skip[...], (SPAN, LANES))

    def level0(j, _):
        for ch in chunks:
            v = dot(near, xc[ch, j])
            for p in range(gc):
                at = j * groups + ch * gc + p
                cols = pl.ds(pl.multiple_of(at * LANES, LANES), LANES)
                o0[:, cols] = (
                    spread(rows[0], 2 * at) * v[:, p * LANES:(p + 1) * LANES]
                    + spread(gain, 2 * at) * x[:, cols].astype(F32)
                )
        return 0

    lax.fori_loop(0, nh, level0, 0)

    for j in y_round:
        move_tau(j, j).wait_recv()
    line = tau[0]
    for j in range(1, ny):
        line = line + tau[j]
    lt[z] = line

    def send_lt(i):
        return remote(lt.at[z], lt.at[z], lts.at[0, z + i], lts.at[1, z], to_z(z + i))

    def recv_lt(i):
        return remote(lt.at[z], lt.at[z - i], lts.at[0, z], lts.at[1, z - i], to_z(z - i))

    for i in range(1, nz):
        @pl.when(z + i < nz)
        def _():
            send_lt(i).start()

    offs = [0]
    for m in range(hbits):
        offs.append(offs[-1] + (nh >> (m + 1)))

    def fold(ch):
        def one(p, _):
            cols = pl.ds(pl.multiple_of(p * LANES, LANES), LANES)
            cur = [sg[g, :, cols] for g in range(nh)]
            dec = [auxr[g, pl.ds(ch * gc + p, 1), :] for g in range(nh)]
            for m in range(hbits):
                new, new_dec = [], []
                for i in range(len(cur) // 2):
                    lbs[ch, offs[m] + i, :, cols] = cur[2 * i].astype(BF16)
                    new.append(cur[2 * i] * jnp.exp(dec[2 * i + 1]) + cur[2 * i + 1])
                    new_dec.append(dec[2 * i] + dec[2 * i + 1])
                cur, dec = new, new_dec
            for r in range(SPLIT):
                sb[ch, p * SPLIT + r] = cur[0][r * rp:(r + 1) * rp].astype(BF16)
            return 0

        lax.fori_loop(0, gc, one, 0)

    def move_r1(ch, j, src):
        return remote(
            sb.at[ch, pl.ds(j * up, up)], r1.at[ch, src],
            r1s.at[0, ch, j], r1s.at[1, ch, src], to_y(j),
        )

    def move_l0(ch, j):
        return remote(sb.at[ch], yb.at[ch, 0], l0s.at[0, ch], l0s.at[1, ch], to_y(j))

    for ch in chunks:
        sg[hd] = dot_t(br[hd], xr[ch, hd])
        for j in reversed(heads_round):
            if ch == 0:
                move_b(j, j).wait_recv()
            move_x(ch, j, j).wait_recv()
            sg[j] = dot_t(br[j], xr[ch, j])
        fold(ch)
        for j in y_round:
            move_r1(ch, j, y).start()

        @pl.when(lax.rem(y, 2) == 0)
        def _():
            move_l0(ch, y + 1).start()

        for q in range(up):
            r1[ch, y, q] = sb[ch, y * up + q]
    for j in heads_round:
        move_c(j, hd).start()

    def weigh(l, cols, g0, g1):
        w = dot(oh[g0 * SPAN:g1 * SPAN, :], te[l, :, cols]).astype(BF16)
        for t in range(g0 // 2, g1 // 2):
            we[l, t, :, cols] = w[(2 * t - g0) * SPAN:(2 * t + 2 - g0) * SPAN]

    for l in range(nlev):
        for i in range(0, groups * LANES, TILE):
            if l < hbits and l > 0:
                for g in range(2 << l >> 1, nh, 2 << l):
                    weigh(l, slice(i, i + TILE), g, g + (1 << l))
            else:
                weigh(l, slice(i, i + TILE), 0, nh)

    for i in range(1, nz):
        @pl.when(z - i >= 0)
        def _():
            recv_lt(i).wait_recv()

    yoffs = [0]
    for m in range(1, ybits):
        yoffs.append(yoffs[-1] + (ny >> (m + 1)))

    def row_of(ch, q):
        return pl.ds(ch * gc + lax.div(y * up + q, SPLIT), 1)

    def send_r2(ch, i):
        return remote(
            tz.at[ch], r2.at[ch, z], r2s.at[0, ch, z + i], r2s.at[1, ch, z], to_z(z + i)
        )

    def recv_r2(ch, i):
        return remote(
            tz.at[ch], r2.at[ch, z - i], r2s.at[0, ch, z], r2s.at[1, ch, z - i], to_z(z - i)
        )

    def move_yb(ch, m, j, src):
        return remote(
            pb.at[ch, yoffs[m - 1] + lax.div(j, 2 << m)], yb.at[ch, m, pl.ds(src * up, up)],
            ys.at[0, ch, m, j], ys.at[1, ch, m, src], to_y(j),
        )

    for ch in chunks:
        for j in y_round:
            move_r1(ch, j, j).wait_recv()
        for q in range(up):
            cur = [r1[ch, j, q].astype(F32) for j in range(ny)]
            dec = [tau[j, row_of(ch, q), :] for j in range(ny)]
            for m in range(ybits):
                new, new_dec = [], []
                for i in range(len(cur) // 2):
                    if m:
                        pb[ch, yoffs[m - 1] + i, q] = cur[2 * i].astype(BF16)
                    new.append(cur[2 * i] * jnp.exp(dec[2 * i + 1]) + cur[2 * i + 1])
                    new_dec.append(dec[2 * i] + dec[2 * i + 1])
                cur, dec = new, new_dec
            r2[ch, z, q] = cur[0].astype(BF16)
            tz[ch, q] = cur[0].astype(BF16)
        for i in range(1, nz):
            @pl.when(z + i < nz)
            def _():
                send_r2(ch, i).start()
        for m in range(1, ybits):
            for j in y_round:
                @pl.when(bit(j, m))
                def _():
                    move_yb(ch, m, j, y).start()

            @pl.when(bit(y, m))
            def _():
                for q in range(up):
                    yb[ch, m, y * up + q] = pb[ch, yoffs[m - 1] + lax.div(y, 2 << m), q]

    for j in heads_round:
        move_c(j, j).wait_recv()

    def cpair(t):
        return cr[pl.ds(2 * t, 2)].reshape(2 * SPAN, STATE)

    def scaled(v, row0, row1):
        return jnp.concatenate([v[:SPAN] * row0, v[SPAN:] * row1], axis=0)

    def gap_rows(lo, g):
        gap = jnp.zeros((groups, LANES), F32)
        for before in range(lo, g):
            gap = gap + auxr[before, 0:groups, :]
        return jnp.exp(gap)

    def wide_rows(tile, ch, cols):
        at = [ch * gc + i // LANES for i in range(cols.start, cols.stop, LANES)]
        return jnp.concatenate([tile[i:i + 1, :] for i in at], axis=1)

    def inner(ch):
        for t in range(nh // 2):
            cp = cpair(t)
            for cols in tiles:
                full = slice(ch * wc + cols.start, ch * wc + cols.stop)
                v = dot(cp[SPAN:], lbs[ch, t, :, cols]) * we[0, t, SPAN:, full].astype(F32)
                acc = None
                for m in range(1, hbits):
                    if not 2 * t >> m & 1:
                        continue
                    lo = 2 * t >> m << m
                    term = we[m, t, :, full].astype(F32) * dot(
                        cp, lbs[ch, offs[m] + (2 * t >> (m + 1)), :, cols]
                    )
                    term = scaled(
                        term,
                        wide_rows(gap_rows(lo, 2 * t), ch, cols),
                        wide_rows(gap_rows(lo, 2 * t + 1), ch, cols),
                    )
                    acc = term if acc is None else acc + term
                if acc is None:
                    li[t, :SPAN, full] = jnp.zeros((SPAN, TILE), F32)
                    li[t, SPAN:, full] = v
                else:
                    li[t, :SPAN, full] = acc[:SPAN]
                    li[t, SPAN:, full] = acc[SPAN:] + v

    for ch in chunks:
        inner(ch)

    right, left = lax.rem(y + 1, ny), lax.rem(y + ny - 1, ny)
    steps = (ny // 2, ny - 1 - ny // 2)

    def hop(ch, m, way, s):
        own = lax.rem(y + ny - s, ny) if way == 0 else lax.rem(y + s, ny)
        part = zb.at[ch, m, pl.ds(own * up, up)]
        return remote(
            part, part, ags.at[0, ch, m, way, s], ags.at[1, ch, m, way, s],
            to_y(right if way == 0 else left),
        )

    def landed(ch, m, way, s):
        own = lax.rem(y + ny - s - 1, ny) if way == 0 else lax.rem(y + s + 1, ny)
        part = zb.at[ch, m, pl.ds(own * up, up)]
        return remote(
            part, part, ags.at[0, ch, m, way, s], ags.at[1, ch, m, way, s],
            to_y(left if way == 0 else right),
        )

    def pass_on(ch, s):
        for m in range(zbits):
            @pl.when(bit(z, m))
            def _():
                for way in range(2):
                    if s < steps[way]:
                        if s:
                            landed(ch, m, way, s - 1).wait_recv()
                        hop(ch, m, way, s).start()

    def before_y(lo):
        gap = jnp.zeros((groups, LANES), F32)
        for j in range(ny):
            gap = gap + jnp.where(jnp.logical_and(j >= lo, j < y), tau[j], 0.0)
        return gap

    def before_z(lo):
        gap = jnp.zeros((groups, LANES), F32)
        for j in range(nz):
            gap = gap + jnp.where(jnp.logical_and(j >= lo, j < z), lt[j], 0.0)
        return gap

    def put(ch, slot, part, gap):
        scale = jnp.exp(gap)
        for p in range(gc):
            for r in range(SPLIT):
                bks[ch, slot, r * rp:(r + 1) * rp, p * LANES:(p + 1) * LANES] = (
                    part[p * SPLIT + r].astype(F32) * scale[ch * gc + p:ch * gc + p + 1, :]
                ).astype(BF16)

    def put_y(ch):
        for m in range(ybits):
            @pl.when(bit(y, m))
            def _():
                if m == 0:
                    move_l0(ch, y - 1).wait_recv()
                else:
                    for j in y_round:
                        move_yb(ch, m, j, j).wait_recv()
                put(ch, m, yb.at[ch, m], before_y(lax.div(y, 1 << m) * (1 << m)))

            @pl.when(jnp.logical_not(bit(y, m)))
            def _():
                bks[ch, m] = jnp.zeros((STATE, wc), BF16)

    def put_z(ch):
        for m in range(zbits):
            @pl.when(bit(z, m))
            def _():
                for way in range(2):
                    if steps[way]:
                        landed(ch, m, way, steps[way] - 1).wait_recv()
                put(
                    ch, ybits + m, zb.at[ch, m],
                    before_y(0) + before_z(lax.div(z, 1 << m) * (1 << m)),
                )

            @pl.when(jnp.logical_not(bit(z, m)))
            def _():
                bks[ch, ybits + m] = jnp.zeros((STATE, wc), BF16)

    def cross(ch, t, cols, levels):
        full = slice(ch * wc + cols.start, ch * wc + cols.stop)
        cp = cpair(t)
        acc = None
        for m in levels:
            term = we[hbits + m, t, :, full].astype(F32) * dot(cp, bks[ch, m, :, cols])
            acc = term if acc is None else acc + term
        acc = scaled(
            acc, wide_rows(pg[2 * t], ch, cols), wide_rows(pg[2 * t + 1], ch, cols)
        )
        return acc + li[t, :, full]

    def cross_y(ch):
        def one(t, _):
            for cols in tiles:
                full = slice(ch * wc + cols.start, ch * wc + cols.stop)
                li[t, :, full] = cross(ch, t, cols, range(ybits))
            return 0

        lax.fori_loop(0, nh // 2, one, 0)

    def cross_z(ch, t):
        for cols in tiles:
            v = cross(ch, t, cols, range(ybits, ybits + zbits)).astype(BF16)
            io[ch, 2 * t, :, cols] = v[:SPAN]
            io[ch, 2 * t + 1, :, cols] = v[SPAN:]

    def return_rows():
        def one(p, _):
            cols = pl.ds(pl.multiple_of(p * LANES, LANES), LANES)
            er[:, cols] = spread(rows[1], 2 * p)
            return 0

        lax.fori_loop(0, HEADS // 2, one, 0, unroll=4)

    for ch in chunks:
        for i in range(1, nz):
            @pl.when(z - i >= 0)
            def _():
                recv_r2(ch, i).wait_recv()
        for m in range(zbits):
            @pl.when(bit(z, m))
            def _():
                base = lax.div(z, 1 << m) * (1 << m)
                for q in range(up):
                    acc = r2[ch, base - 1, q].astype(F32)
                    gap = lt[base - 1, row_of(ch, q), :]
                    for i in range(2, (1 << m) + 1):
                        acc = acc + r2[ch, base - i, q].astype(F32) * jnp.exp(gap)
                        gap = gap + lt[base - i, row_of(ch, q), :]
                    zb[ch, m, y * up + q] = acc.astype(BF16)
        pass_on(ch, 0)
    return_rows()
    for s in range(1, steps[0]):
        for ch in chunks:
            pass_on(ch, s)
        if s - 1 < CHUNKS:
            put_y(s - 1)
            cross_y(s - 1)
    for ch in range(max(steps[0] - 1, 0), CHUNKS):
        put_y(ch)
        cross_y(ch)

    for ch in chunks:
        put_z(ch)
        for i, t in enumerate(chips_round):
            cross_z(ch, t)
            for j in heads_round[2 * i:2 * i + 2]:
                move_o(ch, j, hd).start()
        cross_z(ch, chip)
        move_o(ch, heads_round[-1], hd).start()
        ir[ch, hd] = io[ch, hd]

    def finish(ch, j):
        def one(p, _):
            at = j * groups + ch * gc + p
            cols = pl.ds(pl.multiple_of(at * LANES, LANES), LANES)
            part = pl.ds(pl.multiple_of(p * LANES, LANES), LANES)
            out[:, cols] = (
                o0[:, cols] + er[:, cols] * ir[ch, j, :, part].astype(F32)
            ).astype(BF16)
            return 0

        lax.fori_loop(0, gc, one, 0, unroll=4)

    for ch in chunks:
        finish(ch, hd)
        for j in heads_round[::-1]:
            move_o(ch, j, j).wait_recv()
            finish(ch, j)

    for j in heads_round:
        move_a(j, hd).wait_send()
        move_b(j, hd).wait_send()
        move_c(j, hd).wait_send()
        for ch in chunks:
            move_x(ch, j, hd).wait_send()
            move_o(ch, j, hd).wait_send()
    for j in y_round:
        move_tau(j, y).wait_send()
        for ch in chunks:
            move_r1(ch, j, y).wait_send()
        for m in range(1, ybits):
            @pl.when(bit(j, m))
            def _():
                for ch in chunks:
                    move_yb(ch, m, j, y).wait_send()

    @pl.when(lax.rem(y, 2) == 0)
    def _():
        for ch in chunks:
            move_l0(ch, y + 1).wait_send()

    for i in range(1, nz):
        @pl.when(z + i < nz)
        def _():
            send_lt(i).wait_send()
            for ch in chunks:
                send_r2(ch, i).wait_send()
    for s in range(steps[0]):
        for m in range(zbits):
            @pl.when(bit(z, m))
            def _():
                for ch in chunks:
                    for way in range(2):
                        if s < steps[way]:
                            hop(ch, m, way, s).wait_send()


def on_device(nh, ny, nz, token_inputs, state_in, state_out, log_decay, token_codes, table, gain):
    hl = HEADS // nh
    groups = hl // 2
    gc = groups // CHUNKS
    units = gc * SPLIT
    up = units // ny
    rp = STATE // SPLIT
    wide = hl * HEAD_DIM
    wc = wide // CHUNKS
    hbits, ybits, zbits = bits_of(nh), bits_of(ny), bits_of(nz)
    nlev = hbits + ybits + zbits
    vm = pltpu.VMEM
    sem = pltpu.SemaphoreType.DMA
    pieces = max(sum(ny >> (m + 1) for m in range(1, ybits)), 1)
    nc = CHUNKS
    zb = max(zbits, 1)
    return pl.pallas_call(
        functools.partial(kernel, nh, ny, nz),
        out_shape=jax.ShapeDtypeStruct((SPAN, HEADS * HEAD_DIM), BF16),
        in_specs=[pl.BlockSpec(memory_space=pltpu.VMEM)] * 7,
        out_specs=pl.BlockSpec(memory_space=pltpu.VMEM),
        scratch_shapes=[
            vm((nc, nh, SPAN, wc), BF16),
            vm((nc, nh, SPAN, wc), BF16),
            vm((nh, SPAN, STATE), BF16),
            vm((nh, SPAN, STATE), BF16),
            vm((nh, groups + 8, LANES), F32),
            vm((nh, groups + 8, LANES), F32),
            vm((SPAN, HEADS * HEAD_DIM), F32),
            vm((SPAN, HEADS * HEAD_DIM), F32),
            vm((2, SPAN, LANES), F32),
            vm((nlev, CODES, wide), BF16),
            vm((nh * SPAN, CODES), BF16),
            vm((nlev, nh // 2, 2 * SPAN, wide), BF16),
            vm((nh, STATE, wc), F32),
            vm((nc, nh - 1, STATE, wc), BF16),
            vm((nh // 2, 2 * SPAN, wide), F32),
            vm((nc, units, rp, LANES), BF16),
            vm((nc, ny, up, rp, LANES), BF16),
            vm((nc, pieces, up, rp, LANES), BF16),
            vm((nc, up, rp, LANES), BF16),
            vm((nc, nz, up, rp, LANES), BF16),
            vm((nc, ybits, units, rp, LANES), BF16),
            vm((nc, zb, units, rp, LANES), BF16),
            vm((nc, ybits + zbits, STATE, wc), BF16),
            vm((ny, groups, LANES), F32),
            vm((nz, groups, LANES), F32),
            vm((nh, groups, LANES), F32),
            vm((nc, nh, SPAN, wc), BF16),
            vm((nc, nh, SPAN, wc), BF16),
            sem((2, nc, nh)),
            sem((2, nh)),
            sem((2, nh)),
            sem((2, nh)),
            sem((2, ny)),
            sem((2, nz)),
            sem((2, nc, ny)),
            sem((2, nc)),
            sem((2, nc, max(ybits, 1), ny)),
            sem((2, nc, nz)),
            sem((2, nc, zb, 2, max(ny // 2, 1))),
            sem((2, nc, nh)),
        ],
        compiler_params=pltpu.CompilerParams(
            collective_id=0, has_side_effects=True, vmem_limit_bytes=VMEM_LIMIT
        ),
    )(
        token_inputs, state_in, state_out, log_decay,
        token_codes.reshape(1, SPAN), table, gain.reshape(1, HEADS),
    )


def solution(mesh, ny=NY):
    nh = mesh.shape["head"]
    nz = mesh.shape["ctx"] // ny
    return jax.shard_map(
        functools.partial(on_device, nh, ny, nz),
        mesh=mesh,
        in_specs=(
            P(("ctx", "head"), None),
            P(("ctx", "head"), None),
            P(("ctx", "head"), None),
            P(("ctx", "head"), None),
            P(("ctx", "head")),
            P(),
            P(),
        ),
        out_specs=P(("ctx", "head"), None),
        check_vma=False,
    )
```

time: 80.5 us -> 77.3 us (0.960)
  Pallas kernels: 78.1 us -> 71.1 us
  local copies, waits for them, and re-layouts: 2.26 us -> 5.94 us
    pallas_call x1, Pallas kernels: 78.1 us -> 71.1 us  [on_device(): pl.pallas_call(functools.partial(kernel, nh, ny, nz), out_shape=jax.Shape...]
    unnamed x1 -> x15, local copies, waits for them, and re-layouts: 2.26 us -> 5.94 us
where the time goes in v2:
time: 77.3 us; the launch traced here: 77 us
  Pallas kernels  71.1 us (92%)
  local copies, waits for them, and re-layouts  5.94 us (8%)
    pallas_call x1, Pallas kernels, on_device(): pl.pallas_call(functools.partial(kernel, nh, ny, nz), out_shape=jax.Shape...  71.1 us
    unnamed x15, local copies, waits for them, and re-layouts  5.94 us

profile of v2, /device:TPU:65, one launch (start us, length us, event | category | flops | bytes accessed | tf_op | source)
XLA Modules:
  0.0 77.0 jit_solution(14450754541292599289)
XLA Ops:
  0.0 0.0 copy-start.5
  0.0 0.0 copy-start.6
  0.0 0.7 copy-done.5
  0.7 0.0 copy-done.6
  0.7 0.0 copy-start
  0.7 1.2 %copy-done = bf16[64,8192]{1,0:T(8,128)(2,1)S(1)} copy-done((bf16[64,8192]{1,0:T(8,128)(2,1)S(1)}, bf16[64,8192]{1,0:T(8,128)(2,1)}, u32[]{:S(2)}) %copy-start) | copy-done | bytes 1048600
  1.9 0.0 copy-start.1
  1.9 0.9 %copy-done.1 = bf16[64,1408]{1,0:T(8,128)(2,1)S(1)} copy-done((bf16[64,1408]{1,0:T(8,128)(2,1)S(1)}, bf16[64,1408]{1,0:T(8,128)(2,1)}, u32[]{:S(2)}) %copy-start.1) | copy-done | bytes 180248
  2.8 0.0 copy-start.2
  2.8 0.7 copy-done.2
  3.5 0.0 copy-start.3
  3.5 0.7 copy-done.3
  4.3 0.0 copy-start.4
  4.3 0.7 copy-done.4
  5.0 71.1 %shard_map.73 = bf16[64,8192]{1,0:T(8,128)(2,1)S(1)} custom-call(bf16[64,8192]{1,0:T(8,128)(2,1)S(1)} %copy-done, bf16[64,128]{1,0:T(8,128)(2,1)S(1)} %copy-done.2, bf16[64,128]{1,0:T(8,128)(2,1)S(1)} %copy-done.3, bf16[64,128]{1,0:T(8,128)(2,1)S(1)} %copy-done.4, s32[1,64]{1,0:T(1,128)S(1)} %bitcast.2, bf16[64,1408]{1,0:T(8,128)(2,1)S(1)} %copy-done.1, ...), custom_call_target="tpu_custom_call" | custom-call | tf_op jit(solution)/shard_map/pallas_call | solution.py:650
  76.0 1.0 %copy.9 = bf16[64,8192]{1,0:T(8,128)(2,1)} copy(bf16[64,8192]{1,0:T(8,128)(2,1)S(1)} %shard_map.73) | data formatting | bytes 2097152
Async XLA Ops:
  0.0 0.7 copy-start.5
  0.0 0.7 copy-start.6
  0.7 1.2 %copy-start = (bf16[64,8192]{1,0:T(8,128)(2,1)S(1)}, bf16[64,8192]{1,0:T(8,128)(2,1)}, u32[]{:S(2)}) copy-start(bf16[64,8192]{1,0:T(8,128)(2,1)} %x.1) | copy-start | bytes 3145732
  1.9 0.9 %copy-start.1 = (bf16[64,1408]{1,0:T(8,128)(2,1)S(1)}, bf16[64,1408]{1,0:T(8,128)(2,1)}, u32[]{:S(2)}) copy-start(bf16[64,1408]{1,0:T(8,128)(2,1)} %tab.1) | copy-start | bytes 540676
  2.8 0.7 copy-start.2
  3.5 0.7 copy-start.3
  4.3 0.7 copy-start.4

commit v3 on v2

--- a/solution.py
+++ b/solution.py
@@ -47,10 +47,11 @@
 
 def kernel(
     nh, ny, nz,
-    x, b, c, d, codes, tab, skip, out,
+    x_in, b_in, c_in, d_in, codes_in, tab_in, skip_in, out,
+    x, d, codes, tab, skip,
     xc, xr, br, cr, aux, auxr, o0, er, rows, te, oh, we, sg, lbs, li,
     sb, r1, pb, tz, r2, yb, zb, bks, tau, lt, pg, io, ir,
-    xs, bs, cs, axs, taus, lts, r1s, l0s, ys, r2s, ags, ios,
+    ins, xs, bs, cs, axs, taus, lts, r1s, l0s, ys, r2s, ags, ios,
 ):
     hl = HEADS // nh
     groups = hl // 2
@@ -105,24 +106,22 @@
     for j in z_round:
         pl.semaphore_signal(barrier, inc=1, device_id=to_z(j), device_id_type=MESH)
 
+    loads = [
+        pltpu.make_async_copy(src, dst, ins.at[i])
+        for i, (src, dst) in enumerate((
+            (d_in, d), (x_in, x), (b_in, br.at[hd]), (c_in, cr.at[hd]),
+            (codes_in, codes), (tab_in, tab), (skip_in, skip),
+        ))
+    ]
+    for load in loads:
+        load.start()
+    b, c = br.at[hd], cr.at[hd]
+
+    loads[0].wait()
     lower = iota((SPAN, SPAN), 0) >= iota((SPAN, SPAN), 1)
     run = dot(jnp.where(lower, 1.0, 0.0).astype(BF16), d[...])
     tot = run[SPAN - 1:SPAN, :]
     fac = jnp.exp(tot - run)
-
-    pairs = HEADS // 2
-    first = 2 * iota((pairs, LANES), 0) + (iota((pairs, LANES), 1) >> 6)
-    tot_pairs = jnp.take_along_axis(
-        jnp.broadcast_to(tot, (pairs, LANES)), first, axis=1, mode="promise_in_bounds"
-    )
-    code_row = codes[...].astype(F32)
-    for j in range(nh):
-        aux[j, 0:groups, :] = tot_pairs[j * groups:(j + 1) * groups, :]
-        aux[j, groups:groups + 8, 0:SPAN] = jnp.broadcast_to(code_row, (8, SPAN))
-        aux[j, groups:groups + 8, SPAN:] = jnp.zeros((8, LANES - SPAN), F32)
-    auxr[hd] = aux[hd]
-    br[hd] = b[...]
-    cr[hd] = c[...]
 
     def carry(ch, j):
         def one(p, _):
@@ -154,17 +153,34 @@
             io.at[ch, j], ir.at[ch, src], ios.at[0, ch, j], ios.at[1, ch, src], to_head(j)
         )
 
+    def share_aux():
+        pairs = HEADS // 2
+        first = 2 * iota((pairs, LANES), 0) + (iota((pairs, LANES), 1) >> 6)
+        tot_pairs = jnp.take_along_axis(
+            jnp.broadcast_to(tot, (pairs, LANES)), first, axis=1, mode="promise_in_bounds"
+        )
+        code_row = codes[...].astype(F32)
+        for j in range(nh):
+            aux[j, 0:groups, :] = tot_pairs[j * groups:(j + 1) * groups, :]
+            aux[j, groups:groups + 8, 0:SPAN] = jnp.broadcast_to(code_row, (8, SPAN))
+            aux[j, groups:groups + 8, SPAN:] = jnp.zeros((8, LANES - SPAN), F32)
+        auxr[hd] = aux[hd]
+        for j in heads_round:
+            move_a(j, hd).start()
+
+    for load in loads[1:]:
+        load.wait()
     carry(0, heads_round[0])
     pl.semaphore_wait(barrier, (nh - 1) + (ny - 1) + (nz - 1))
-    for j in heads_round:
-        move_a(j, hd).start()
-    for j in heads_round:
-        move_b(j, hd).start()
     for ch in chunks:
         for i, j in enumerate(heads_round):
             if i or ch:
                 carry(ch, j)
             move_x(ch, j, hd).start()
+            if ch == 0:
+                move_b(j, hd).start()
+        if ch == 0:
+            share_aux()
     for ch in chunks:
         carry(ch, hd)
         xr[ch, hd] = xc[ch, hd]
@@ -187,6 +203,7 @@
     cols0 = iota((LEVELS * HEADS, LANES), 0)
     lane0 = iota((LEVELS * HEADS, LANES), 1)
     tab0 = dot(tab[...], jnp.where(cols0 == lane0 * LEVELS, 1.0, 0.0).astype(BF16)).astype(BF16)
+    code_row = codes[...].astype(F32)
     code_t = jnp.where(
         jnp.broadcast_to(code_row, (CODES, SPAN)) == iota((CODES, SPAN), 0).astype(F32), 1.0, 0.0
     ).astype(BF16)
@@ -250,6 +267,19 @@
         def _():
             send_lt(i).start()
 
+    def weigh(l, cols, g0, g1):
+        w = dot(oh[g0 * SPAN:g1 * SPAN, :], te[l, :, cols]).astype(BF16)
+        for t in range(g0 // 2, g1 // 2):
+            we[l, t, :, cols] = w[(2 * t - g0) * SPAN:(2 * t + 2 - g0) * SPAN]
+
+    for l in range(nlev):
+        for i in range(0, groups * LANES, TILE):
+            if l < hbits and l > 0:
+                for g in range(2 << l >> 1, nh, 2 << l):
+                    weigh(l, slice(i, i + TILE), g, g + (1 << l))
+            else:
+                weigh(l, slice(i, i + TILE), 0, nh)
+
     offs = [0]
     for m in range(hbits):
         offs.append(offs[-1] + (nh >> (m + 1)))
@@ -301,19 +331,6 @@
     for j in heads_round:
         move_c(j, hd).start()
 
-    def weigh(l, cols, g0, g1):
-        w = dot(oh[g0 * SPAN:g1 * SPAN, :], te[l, :, cols]).astype(BF16)
-        for t in range(g0 // 2, g1 // 2):
-            we[l, t, :, cols] = w[(2 * t - g0) * SPAN:(2 * t + 2 - g0) * SPAN]
-
-    for l in range(nlev):
-        for i in range(0, groups * LANES, TILE):
-            if l < hbits and l > 0:
-                for g in range(2 << l >> 1, nh, 2 << l):
-                    weigh(l, slice(i, i + TILE), g, g + (1 << l))
-            else:
-                weigh(l, slice(i, i + TILE), 0, nh)
-
     for i in range(1, nz):
         @pl.when(z - i >= 0)
         def _():
@@ -342,7 +359,7 @@
             ys.at[0, ch, m, j], ys.at[1, ch, m, src], to_y(j),
         )
 
-    for ch in chunks:
+    def line_sums(ch):
         for j in y_round:
             move_r1(ch, j, j).wait_recv()
         for q in range(up):
@@ -372,6 +389,8 @@
             def _():
                 for q in range(up):
                     yb[ch, m, y * up + q] = pb[ch, yoffs[m - 1] + lax.div(y, 2 << m), q]
+
+    line_sums(0)
 
     for j in heads_round:
         move_c(j, j).wait_recv()
@@ -537,7 +556,7 @@
 
         lax.fori_loop(0, HEADS // 2, one, 0, unroll=4)
 
-    for ch in chunks:
+    def z_sums(ch):
         for i in range(1, nz):
             @pl.when(z - i >= 0)
             def _():
@@ -554,26 +573,39 @@
                         gap = gap + lt[base - i, row_of(ch, q), :]
                     zb[ch, m, y * up + q] = acc.astype(BF16)
         pass_on(ch, 0)
-    return_rows()
-    for s in range(1, steps[0]):
-        for ch in chunks:
-            pass_on(ch, s)
-        if s - 1 < CHUNKS:
-            put_y(s - 1)
-            cross_y(s - 1)
-    for ch in range(max(steps[0] - 1, 0), CHUNKS):
-        put_y(ch)
-        cross_y(ch)
-
-    for ch in chunks:
-        put_z(ch)
-        for i, t in enumerate(chips_round):
-            cross_z(ch, t)
+
+    def give_back(ch, i):
+        if i < len(chips_round):
+            cross_z(ch, chips_round[i])
             for j in heads_round[2 * i:2 * i + 2]:
                 move_o(ch, j, hd).start()
-        cross_z(ch, chip)
-        move_o(ch, heads_round[-1], hd).start()
-        ir[ch, hd] = io[ch, hd]
+        elif i == len(chips_round):
+            cross_z(ch, chip)
+            move_o(ch, heads_round[-1], hd).start()
+            ir[ch, hd] = io[ch, hd]
+
+    z_sums(0)
+    line_sums(1)
+    pass_on(0, 1)
+    return_rows()
+    pass_on(0, 2)
+    put_y(0)
+    cross_y(0)
+    pass_on(0, 3)
+    z_sums(1)
+    put_y(1)
+    cross_y(1)
+    pass_on(1, 1)
+    put_z(0)
+    give_back(0, 0)
+    give_back(0, 1)
+    pass_on(1, 2)
+    give_back(0, 2)
+    give_back(0, 3)
+    pass_on(1, 3)
+    put_z(1)
+    for i in range(4):
+        give_back(1, i)
 
     def finish(ch, j):
         def one(p, _):
@@ -650,9 +682,14 @@
     return pl.pallas_call(
         functools.partial(kernel, nh, ny, nz),
         out_shape=jax.ShapeDtypeStruct((SPAN, HEADS * HEAD_DIM), BF16),
-        in_specs=[pl.BlockSpec(memory_space=pltpu.VMEM)] * 7,
+        in_specs=[pl.BlockSpec(memory_space=pltpu.HBM)] * 7,
         out_specs=pl.BlockSpec(memory_space=pltpu.VMEM),
         scratch_shapes=[
+            vm((SPAN, HEADS * HEAD_DIM), BF16),
+            vm((SPAN, HEADS), BF16),
+            vm((1, SPAN), jnp.int32),
+            vm((CODES, LEVELS * HEADS), BF16),
+            vm((1, HEADS), F32),
             vm((nc, nh, SPAN, wc), BF16),
             vm((nc, nh, SPAN, wc), BF16),
             vm((nh, SPAN, STATE), BF16),
@@ -681,6 +718,7 @@
             vm((nh, groups, LANES), F32),
             vm((nc, nh, SPAN, wc), BF16),
             vm((nc, nh, SPAN, wc), BF16),
+            sem((7,)),
             sem((2, nc, nh)),
             sem((2, nh)),
             sem((2, nh)),
@@ -697,10 +735,13 @@
         compiler_params=pltpu.CompilerParams(
             collective_id=0, has_side_effects=True, vmem_limit_bytes=VMEM_LIMIT
         ),
-    )(
-        token_inputs, state_in, state_out, log_decay,
-        token_codes.reshape(1, SPAN), table, gain.reshape(1, HEADS),
-    )
+    )(*(
+        pltpu.with_memory_space_constraint(v, pltpu.HBM)
+        for v in (
+            token_inputs, state_in, state_out, log_decay,
+            token_codes.reshape(1, SPAN), table, gain.reshape(1, HEADS),
+        )
+    ))
 
 
 def solution(mesh, ny=NY):

time: 77.3 us -> 78.9 us (1.021)
  the two profiles are of different devices: /device:TPU:65 before, /device:TPU:73 now
where the time goes in v3:
time: 78.9 us; the launch traced here: 78.7 us
  Pallas kernels  77.7 us (98%)
  local copies, waits for them, and re-layouts  0.97 us (1%)
    pallas_call x1, Pallas kernels, on_device(): pl.pallas_call(functools.partial(kernel, nh, ny, nz), out_shape=jax.Shape...  77.7 us

profile of v3, /device:TPU:73, one launch (start us, length us, event | category | flops | bytes accessed | tf_op | source)
XLA Modules:
  0.0 78.7 jit_solution(7042210772651766814)
XLA Ops:
  0.0 77.7 %shard_map.73 = bf16[64,8192]{1,0:T(8,128)(2,1)S(1)} custom-call(bf16[64,8192]{1,0:T(8,128)(2,1)} %x_in.1, bf16[64,128]{1,0:T(8,128)(2,1)} %b_in.1, bf16[64,128]{1,0:T(8,128)(2,1)} %c_in.1, bf16[64,128]{1,0:T(8,128)(2,1)} %d_in.1, s32[1,64]{1,0:T(1,128)} %bitcast.2, bf16[64,1408]{1,0:T(8,128)(2,1)} %tab_in.1, f32[1,128]{1,0:T(1,128)} %bitcast.3), custom_call_target="tpu_custom_call" | custom-call | tf_op jit(solution)/shard_map/pallas_call | solution.py:682
  77.7 1.0 %copy.9 = bf16[64,8192]{1,0:T(8,128)(2,1)} copy(bf16[64,8192]{1,0:T(8,128)(2,1)S(1)} %shard_map.73) | data formatting | bytes 2097152

commit v4 on v3

--- a/solution.py
+++ b/solution.py
@@ -50,8 +50,8 @@
     x_in, b_in, c_in, d_in, codes_in, tab_in, skip_in, out,
     x, d, codes, tab, skip,
     xc, xr, br, cr, aux, auxr, o0, er, rows, te, oh, we, sg, lbs, li,
-    sb, r1, pb, tz, r2, yb, zb, bks, tau, lt, pg, io, ir,
-    ins, xs, bs, cs, axs, taus, lts, r1s, l0s, ys, r2s, ags, ios,
+    sb, r1, pb, tz, r2, yb, zb, bks, tau, lt, pg, io, ir, rl,
+    ins, xs, bs, cs, axs, taus, lts, r1s, l0s, ys, r2s, ags, ios, rls, fws,
 ):
     hl = HEADS // nh
     groups = hl // 2
@@ -94,6 +94,11 @@
     for q in chips_round:
         heads_round += [2 * q + core, 2 * q + 1 - core]
     heads_round.append(2 * chip + 1 - core)
+    relayed = nh == 8
+    near_heads = heads_round[2:] if relayed else heads_round
+    far = lax.rem(chip + 2, nh // 2)
+    mid = lax.rem(chip + 1 + 2 * core, nh // 2)
+    helped = 2 * lax.rem(chip + 3 - 2 * core, nh // 2) + core
     y_round = [lax.rem(y + i, ny) for i in range(1, ny)]
     z_round = [lax.rem(z + i, nz) for i in range(1, nz)]
 
@@ -168,38 +173,47 @@
         for j in heads_round:
             move_a(j, hd).start()
 
+    def relay(kind, ch):
+        src = (xc, io)[kind].at[ch, pl.ds(2 * far, 2)]
+        return remote(
+            src, rl.at[kind, ch], rls.at[0, kind, ch], rls.at[1, kind, ch], to_head(2 * mid + core)
+        )
+
+    def forward(kind, ch, f):
+        dst, sems = ((xr, xs), (ir, ios))[kind]
+        return remote(
+            rl.at[kind, ch, f], dst.at[ch, helped], fws.at[kind, ch, f],
+            sems.at[1, ch, helped], to_head(2 * mid + f),
+        )
+
+    def hand_on(kind, ch):
+        if relayed:
+            relay(kind, ch).wait_recv()
+            for f in range(2):
+                forward(kind, ch, f).start()
+
+    def send_far(ch):
+        if relayed:
+            for j in heads_round[:2]:
+                carry(ch, j)
+            relay(0, ch).start()
+
     for load in loads[1:]:
         load.wait()
     carry(0, heads_round[0])
     pl.semaphore_wait(barrier, (nh - 1) + (ny - 1) + (nz - 1))
-    for ch in chunks:
-        for i, j in enumerate(heads_round):
-            if i or ch:
-                carry(ch, j)
-            move_x(ch, j, hd).start()
-            if ch == 0:
-                move_b(j, hd).start()
-        if ch == 0:
-            share_aux()
-    for ch in chunks:
-        carry(ch, hd)
-        xr[ch, hd] = xc[ch, hd]
-
-    for j in heads_round:
-        move_a(j, j).wait_recv()
-    mine = auxr[0, 0:groups, :]
-    for g in range(nh):
-        pg[g] = jnp.exp(mine) if g else jnp.ones((groups, LANES), F32)
-        if g:
-            mine = mine + auxr[g, 0:groups, :]
-    tau[y] = mine
-
-    def move_tau(j, src):
-        return remote(tau.at[y], tau.at[src], taus.at[0, j], taus.at[1, src], to_y(j))
-
-    for j in y_round:
-        move_tau(j, y).start()
-
+    if relayed:
+        carry(0, heads_round[1])
+        relay(0, 0).start()
+    for i, j in enumerate(near_heads):
+        if i or relayed:
+            carry(0, j)
+        move_x(0, j, hd).start()
+        move_b(j, hd).start()
+    for j in heads_round[:len(heads_round) - len(near_heads)]:
+        move_b(j, hd).start()
+    send_far(1)
+    share_aux()
     cols0 = iota((LEVELS * HEADS, LANES), 0)
     lane0 = iota((LEVELS * HEADS, LANES), 1)
     tab0 = dot(tab[...], jnp.where(cols0 == lane0 * LEVELS, 1.0, 0.0).astype(BF16)).astype(BF16)
@@ -221,6 +235,29 @@
                 te[l, :, p * LANES:(p + 1) * LANES] = spread(
                     picked, (l - t * per) * hl + 2 * p
                 ).astype(BF16)
+    hand_on(0, 0)
+    for j in near_heads:
+        carry(1, j)
+        move_x(1, j, hd).start()
+    for ch in chunks:
+        carry(ch, hd)
+        xr[ch, hd] = xc[ch, hd]
+
+    for j in heads_round:
+        move_a(j, j).wait_recv()
+    mine = auxr[0, 0:groups, :]
+    for g in range(nh):
+        pg[g] = jnp.exp(mine) if g else jnp.ones((groups, LANES), F32)
+        if g:
+            mine = mine + auxr[g, 0:groups, :]
+    tau[y] = mine
+
+    def move_tau(j, src):
+        return remote(tau.at[y], tau.at[src], taus.at[0, j], taus.at[1, src], to_y(j))
+
+    for j in y_round:
+        move_tau(j, y).start()
+
     eye = jnp.where(iota((CODES, CODES), 0) == iota((CODES, CODES), 1), 1.0, 0.0).astype(BF16)
     for g in range(nh):
         row = auxr[g, groups:groups + 1, 0:SPAN]
@@ -228,6 +265,23 @@
             jnp.broadcast_to(row, (CODES, SPAN)) == iota((CODES, SPAN), 0).astype(F32), 1.0, 0.0
         ).astype(BF16)
         oh[g * SPAN:(g + 1) * SPAN, :] = dot_t(hot, eye).astype(BF16)
+
+    def weigh(l, cols, g0, g1):
+        w = dot(oh[g0 * SPAN:g1 * SPAN, :], te[l, :, cols]).astype(BF16)
+        for t in range(g0 // 2, g1 // 2):
+            we[l, t, :, cols] = w[(2 * t - g0) * SPAN:(2 * t + 2 - g0) * SPAN]
+
+    for l in range(nlev):
+        for i in range(0, groups * LANES, TILE):
+            if l < hbits and l > 0:
+                for g in range(2 << l >> 1, nh, 2 << l):
+                    weigh(l, slice(i, i + TILE), g, g + (1 << l))
+            else:
+                weigh(l, slice(i, i + TILE), 0, nh)
+
+    hand_on(0, 1)
+    for j in heads_round:
+        move_c(j, hd).start()
 
     scores = lax.dot_general(
         c[...], b[...], (((1,), (1,)), ((), ())), preferred_element_type=F32
@@ -266,19 +320,6 @@
         @pl.when(z + i < nz)
         def _():
             send_lt(i).start()
-
-    def weigh(l, cols, g0, g1):
-        w = dot(oh[g0 * SPAN:g1 * SPAN, :], te[l, :, cols]).astype(BF16)
-        for t in range(g0 // 2, g1 // 2):
-            we[l, t, :, cols] = w[(2 * t - g0) * SPAN:(2 * t + 2 - g0) * SPAN]
-
-    for l in range(nlev):
-        for i in range(0, groups * LANES, TILE):
-            if l < hbits and l > 0:
-                for g in range(2 << l >> 1, nh, 2 << l):
-                    weigh(l, slice(i, i + TILE), g, g + (1 << l))
-            else:
-                weigh(l, slice(i, i + TILE), 0, nh)
 
     offs = [0]
     for m in range(hbits):
@@ -328,8 +369,6 @@
 
         for q in range(up):
             r1[ch, y, q] = sb[ch, y * up + q]
-    for j in heads_round:
-        move_c(j, hd).start()
 
     for i in range(1, nz):
         @pl.when(z - i >= 0)
@@ -442,7 +481,7 @@
         inner(ch)
 
     right, left = lax.rem(y + 1, ny), lax.rem(y + ny - 1, ny)
-    steps = (ny // 2, ny - 1 - ny // 2)
+    steps = (ny - 1 - ny // 2, ny // 2)
 
     def hop(ch, m, way, s):
         own = lax.rem(y + ny - s, ny) if way == 0 else lax.rem(y + s, ny)
@@ -524,6 +563,8 @@
     def cross(ch, t, cols, levels):
         full = slice(ch * wc + cols.start, ch * wc + cols.stop)
         cp = cpair(t)
+        if not levels:
+            return li[t, :, full]
         acc = None
         for m in levels:
             term = we[hbits + m, t, :, full].astype(F32) * dot(cp, bks[ch, m, :, cols])
@@ -577,8 +618,11 @@
     def give_back(ch, i):
         if i < len(chips_round):
             cross_z(ch, chips_round[i])
-            for j in heads_round[2 * i:2 * i + 2]:
-                move_o(ch, j, hd).start()
+            if relayed and i == 0:
+                relay(1, ch).start()
+            else:
+                for j in heads_round[2 * i:2 * i + 2]:
+                    move_o(ch, j, hd).start()
         elif i == len(chips_round):
             cross_z(ch, chip)
             move_o(ch, heads_round[-1], hd).start()
@@ -603,6 +647,7 @@
     give_back(0, 2)
     give_back(0, 3)
     pass_on(1, 3)
+    hand_on(1, 0)
     put_z(1)
     for i in range(4):
         give_back(1, i)
@@ -620,6 +665,8 @@
         lax.fori_loop(0, gc, one, 0, unroll=4)
 
     for ch in chunks:
+        if ch:
+            hand_on(1, ch)
         finish(ch, hd)
         for j in heads_round[::-1]:
             move_o(ch, j, j).wait_recv()
@@ -629,9 +676,15 @@
         move_a(j, hd).wait_send()
         move_b(j, hd).wait_send()
         move_c(j, hd).wait_send()
-        for ch in chunks:
+    for ch in chunks:
+        for j in near_heads:
             move_x(ch, j, hd).wait_send()
             move_o(ch, j, hd).wait_send()
+        if relayed:
+            for kind in range(2):
+                relay(kind, ch).wait_send()
+                for f in range(2):
+                    forward(kind, ch, f).wait_send()
     for j in y_round:
         move_tau(j, y).wait_send()
         for ch in chunks:
@@ -653,7 +706,7 @@
             send_lt(i).wait_send()
             for ch in chunks:
                 send_r2(ch, i).wait_send()
-    for s in range(steps[0]):
+    for s in range(max(steps)):
         for m in range(zbits):
             @pl.when(bit(z, m))
             def _():
@@ -718,6 +771,7 @@
             vm((nh, groups, LANES), F32),
             vm((nc, nh, SPAN, wc), BF16),
             vm((nc, nh, SPAN, wc), BF16),
+            vm((2, nc, 2, SPAN, wc), BF16),
             sem((7,)),
             sem((2, nc, nh)),
             sem((2, nh)),
@@ -731,6 +785,8 @@
             sem((2, nc, nz)),
             sem((2, nc, zb, 2, max(ny // 2, 1))),
             sem((2, nc, nh)),
+            sem((2, 2, nc)),
+            sem((2, nc, 2)),
         ],
         compiler_params=pltpu.CompilerParams(
             collective_id=0, has_side_effects=True, vmem_limit_bytes=VMEM_LIMIT

time: 78.9 us -> 80.8 us (1.024)
  Pallas kernels: 77.7 us -> 79.6 us
    pallas_call x1, Pallas kernels: 77.7 us -> 79.6 us  [on_device(): pl.pallas_call(functools.partial(kernel, nh, ny, nz), out_shape=jax.Shape...]
where the time goes in v4:
time: 80.8 us; the launch traced here: 80.6 us
  Pallas kernels  79.6 us (99%)
  local copies, waits for them, and re-layouts  0.97 us (1%)
    pallas_call x1, Pallas kernels, on_device(): pl.pallas_call(functools.partial(kernel, nh, ny, nz), out_shape=jax.Shape...  79.6 us

profile of v4, /device:TPU:73, one launch (start us, length us, event | category | flops | bytes accessed | tf_op | source)
XLA Modules:
  0.0 80.6 jit_solution(6297345452065330403)
XLA Ops:
  0.0 79.6 %shard_map.73 = bf16[64,8192]{1,0:T(8,128)(2,1)S(1)} custom-call(bf16[64,8192]{1,0:T(8,128)(2,1)} %x_in.1, bf16[64,128]{1,0:T(8,128)(2,1)} %b_in.1, bf16[64,128]{1,0:T(8,128)(2,1)} %c_in.1, bf16[64,128]{1,0:T(8,128)(2,1)} %d_in.1, s32[1,64]{1,0:T(1,128)} %bitcast.2, bf16[64,1408]{1,0:T(8,128)(2,1)} %tab_in.1, f32[1,128]{1,0:T(1,128)} %bitcast.3), custom_call_target="tpu_custom_call" | custom-call | tf_op jit(solution)/shard_map/pallas_call | solution.py:735
  79.6 1.0 %copy.9 = bf16[64,8192]{1,0:T(8,128)(2,1)} copy(bf16[64,8192]{1,0:T(8,128)(2,1)S(1)} %shard_map.73) | data formatting | bytes 2097152

commit v5 on v3

--- a/solution.py
+++ b/solution.py
@@ -26,6 +26,10 @@
 
 def bits_of(n):
     return n.bit_length() - 1
+
+
+def far_first(n):
+    return sorted(range(1, n), key=lambda i: -min(i, n - i))
 
 
 def dot(a, b):
@@ -94,7 +98,7 @@
     for q in chips_round:
         heads_round += [2 * q + core, 2 * q + 1 - core]
     heads_round.append(2 * chip + 1 - core)
-    y_round = [lax.rem(y + i, ny) for i in range(1, ny)]
+    y_round = [lax.rem(y + i, ny) for i in far_first(ny)]
     z_round = [lax.rem(z + i, nz) for i in range(1, nz)]
 
     lt[...] = jnp.zeros_like(lt)
@@ -181,6 +185,8 @@
                 move_b(j, hd).start()
         if ch == 0:
             share_aux()
+    for j in heads_round:
+        move_c(j, hd).start()
     for ch in chunks:
         carry(ch, hd)
         xr[ch, hd] = xc[ch, hd]
@@ -322,14 +328,8 @@
         for j in y_round:
             move_r1(ch, j, y).start()
 
-        @pl.when(lax.rem(y, 2) == 0)
-        def _():
-            move_l0(ch, y + 1).start()
-
         for q in range(up):
             r1[ch, y, q] = sb[ch, y * up + q]
-    for j in heads_round:
-        move_c(j, hd).start()
 
     for i in range(1, nz):
         @pl.when(z - i >= 0)
@@ -375,11 +375,17 @@
                 cur, dec = new, new_dec
             r2[ch, z, q] = cur[0].astype(BF16)
             tz[ch, q] = cur[0].astype(BF16)
-        for i in range(1, nz):
+        for i in far_first(nz):
             @pl.when(z + i < nz)
             def _():
                 send_r2(ch, i).start()
-        for m in range(1, ybits):
+
+    def share_y(ch, m):
+        if m == 0:
+            @pl.when(lax.rem(y, 2) == 0)
+            def _():
+                move_l0(ch, y + 1).start()
+        elif m < ybits:
             for j in y_round:
                 @pl.when(bit(j, m))
                 def _():
@@ -391,6 +397,9 @@
                     yb[ch, m, y * up + q] = pb[ch, yoffs[m - 1] + lax.div(y, 2 << m), q]
 
     line_sums(0)
+    for m in range(3):
+        share_y(0, m)
+    line_sums(1)
 
     for j in heads_round:
         move_c(j, j).wait_recv()
@@ -442,7 +451,7 @@
         inner(ch)
 
     right, left = lax.rem(y + 1, ny), lax.rem(y + ny - 1, ny)
-    steps = (ny // 2, ny - 1 - ny // 2)
+    steps = (ny - 1 - ny // 2, ny // 2)
 
     def hop(ch, m, way, s):
         own = lax.rem(y + ny - s, ny) if way == 0 else lax.rem(y + s, ny)
@@ -585,24 +594,26 @@
             ir[ch, hd] = io[ch, hd]
 
     z_sums(0)
-    line_sums(1)
+    share_y(1, 0)
+    return_rows()
     pass_on(0, 1)
-    return_rows()
-    pass_on(0, 2)
+    share_y(1, 1)
     put_y(0)
     cross_y(0)
+    pass_on(0, 2)
+    share_y(1, 2)
+    z_sums(1)
     pass_on(0, 3)
-    z_sums(1)
+    pass_on(1, 1)
     put_y(1)
     cross_y(1)
-    pass_on(1, 1)
+    pass_on(1, 2)
     put_z(0)
     give_back(0, 0)
     give_back(0, 1)
-    pass_on(1, 2)
+    pass_on(1, 3)
     give_back(0, 2)
     give_back(0, 3)
-    pass_on(1, 3)
     put_z(1)
     for i in range(4):
         give_back(1, i)
@@ -653,7 +664,7 @@
             send_lt(i).wait_send()
             for ch in chunks:
                 send_r2(ch, i).wait_send()
-    for s in range(steps[0]):
+    for s in range(max(steps)):
         for m in range(zbits):
             @pl.when(bit(z, m))
             def _():

time: 78.9 us -> 74.1 us (0.939)
  the two profiles are of different devices: /device:TPU:73 before, /device:TPU:75 now
where the time goes in v5:
time: 74.1 us; the launch traced here: 74 us
  Pallas kernels  73 us (99%)
  local copies, waits for them, and re-layouts  0.97 us (1%)
    pallas_call x1, Pallas kernels, on_device(): pl.pallas_call(functools.partial(kernel, nh, ny, nz), out_shape=jax.Shape...  73 us

profile of v5, /device:TPU:75, one launch (start us, length us, event | category | flops | bytes accessed | tf_op | source)
XLA Modules:
  0.0 74.0 jit_solution(3402279931452326876)
XLA Ops:
  0.0 73.0 %shard_map.73 = bf16[64,8192]{1,0:T(8,128)(2,1)S(1)} custom-call(bf16[64,8192]{1,0:T(8,128)(2,1)} %x_in.1, bf16[64,128]{1,0:T(8,128)(2,1)} %b_in.1, bf16[64,128]{1,0:T(8,128)(2,1)} %c_in.1, bf16[64,128]{1,0:T(8,128)(2,1)} %d_in.1, s32[1,64]{1,0:T(1,128)} %bitcast.2, bf16[64,1408]{1,0:T(8,128)(2,1)} %tab_in.1, f32[1,128]{1,0:T(1,128)} %bitcast.3), custom_call_target="tpu_custom_call" | custom-call | tf_op jit(solution)/shard_map/pallas_call | solution.py:693
  73.0 1.0 %copy.9 = bf16[64,8192]{1,0:T(8,128)(2,1)} copy(bf16[64,8192]{1,0:T(8,128)(2,1)S(1)} %shard_map.73) | data formatting | bytes 2097152

commit v6 on v5

--- a/solution.py
+++ b/solution.py
@@ -605,15 +605,15 @@
     z_sums(1)
     pass_on(0, 3)
     pass_on(1, 1)
-    put_y(1)
-    cross_y(1)
-    pass_on(1, 2)
     put_z(0)
     give_back(0, 0)
     give_back(0, 1)
-    pass_on(1, 3)
+    pass_on(1, 2)
     give_back(0, 2)
     give_back(0, 3)
+    put_y(1)
+    cross_y(1)
+    pass_on(1, 3)
     put_z(1)
     for i in range(4):
         give_back(1, i)

time: 74.1 us -> 73.8 us (level)
  the two profiles are of different devices: /device:TPU:75 before, /device:TPU:91 now
where the time goes in v6:
time: 73.8 us; the launch traced here: 73.7 us
  Pallas kernels  72.7 us (99%)
  local copies, waits for them, and re-layouts  0.97 us (1%)
    pallas_call x1, Pallas kernels, on_device(): pl.pallas_call(functools.partial(kernel, nh, ny, nz), out_shape=jax.Shape...  72.7 us

profile of v6, /device:TPU:91, one launch (start us, length us, event | category | flops | bytes accessed | tf_op | source)
XLA Modules:
  0.0 73.7 jit_solution(1050643792058886813)
XLA Ops:
  0.0 72.7 %shard_map.73 = bf16[64,8192]{1,0:T(8,128)(2,1)S(1)} custom-call(bf16[64,8192]{1,0:T(8,128)(2,1)} %x_in.1, bf16[64,128]{1,0:T(8,128)(2,1)} %b_in.1, bf16[64,128]{1,0:T(8,128)(2,1)} %c_in.1, bf16[64,128]{1,0:T(8,128)(2,1)} %d_in.1, s32[1,64]{1,0:T(1,128)} %bitcast.2, bf16[64,1408]{1,0:T(8,128)(2,1)} %tab_in.1, f32[1,128]{1,0:T(1,128)} %bitcast.3), custom_call_target="tpu_custom_call" | custom-call | tf_op jit(solution)/shard_map/pallas_call | solution.py:693
  72.7 1.0 %copy.9 = bf16[64,8192]{1,0:T(8,128)(2,1)} copy(bf16[64,8192]{1,0:T(8,128)(2,1)S(1)} %shard_map.73) | data formatting | bytes 2097152
